TPU v7x, 128 devices: a whole 4x4x4 slice. The times are simulated.
128 devices in a mesh: grp: 2 (over y_hi), dev: 64 (over x, z, y_lo, core).
Axes of the slice: x: 4, y: 4 (y_hi: 2, y_lo: 2; y = y_hi * 2 + y_lo), z: 4, core: 2. Of those that a mesh axis runs over, the one named last changes fastest.
Arguments:
- multipoles: float32 [2, 384, 41472], P(None, ('grp', 'dev')), may hold values from -6 to 6
- derivatives: float32 [384, 512, 289], P(None, ('grp', 'dev')), may hold values from -0.6666667 to 0.6666667
Outputs:
- taylors: float32 [2, 384, 41472], P(None, ('grp', 'dev'))
All inputs are finite; a program needn't handle non-finite values.
Results may differ from a plain program's by a relative error of at most 0.0001.
Values sent between devices are 32-bit elements; how exact they have to be, the bound alone decides.
A program may use at most 192 MiB of HBM per device.

v0:
```python
import math

import jax
import jax.numpy as jnp
import numpy as np
from jax import lax
from jax.sharding import PartitionSpec as P

ORDER = 8


def reduced_terms(highest):
    listed = []
    for total in range(highest + 1):
        for upper in range(min(total, 1) + 1):
            for first in range(total - upper, -1, -1):
                listed.append((first, total - upper - first, upper))
    return listed


def coupling_matrix(order):
    lower = reduced_terms(order)
    higher = reduced_terms(2 * order)
    where = {}
    for place, triple in enumerate(higher):
        where[triple] = place
    count = len(lower)
    table = np.zeros((len(higher), count * count), np.float32)
    for left, one in enumerate(lower):
        for right, other in enumerate(lower):
            summed = (one[0] + other[0], one[1] + other[1], one[2] + other[2])
            column = left * count + right
            if summed[2] <= 1:
                table[where[summed], column] += 1.0
            else:
                table[where[summed[0] + 2, summed[1], 0], column] -= 1.0
                table[where[summed[0], summed[1] + 2, 0], column] -= 1.0
    return table


def dft_tables(length, positions):
    kvalues = jnp.arange(length, dtype=jnp.int32)
    phase = kvalues[:, None] * positions[None, :] % length
    angle = 2.0 * math.pi / length * phase.astype(jnp.float32)
    factor = 1.0 / math.sqrt(length)
    cosine = jnp.cos(angle) * factor
    sine = jnp.sin(angle) * factor
    forward = jnp.stack([jnp.stack([cosine, sine], 1), jnp.stack([-sine, cosine], 1)], 0)
    inverse = jnp.stack([jnp.stack([cosine.T, -sine.T], 1), jnp.stack([sine.T, cosine.T], 1)], 0)
    return (forward, inverse)


def contract_rows(deriv_rows, spectrum, comp_count):
    table = jnp.asarray(coupling_matrix(ORDER))
    total = deriv_rows.shape[0]
    width = math.gcd(total, 768)
    count = total // width

    def step(index, result):
        start = (index * width).astype(jnp.int32)
        deriv_block = lax.dynamic_slice_in_dim(deriv_rows, start, width, 0)
        coupling = jnp.dot(deriv_block, table, precision=lax.Precision.HIGHEST)
        coupling = coupling.reshape(width, comp_count, comp_count)
        moment_block = lax.dynamic_slice_in_dim(spectrum, start, width, 1)
        block_out = jnp.einsum(
            "pab,rpb->rpa", coupling, moment_block, precision=lax.Precision.HIGHEST
        )
        return lax.dynamic_update_slice_in_dim(result, block_out, start, 1)

    return lax.fori_loop(0, count, step, jnp.zeros(spectrum.shape, spectrum.dtype))


def convolve_group(multipoles, derivatives):
    outer = lax.axis_size("grp")
    inner = lax.axis_size("dev")
    local_rows = multipoles.shape[1]
    length = local_rows * outer * inner
    comp_count = (ORDER + 1) ** 2
    deriv_count = derivatives.shape[2]
    mode_count = derivatives.shape[1]
    row_index = jnp.arange(length, dtype=jnp.int32)
    slab_rows = lax.all_to_all(multipoles, ("grp", "dev"), split_axis=2, concat_axis=1, tiled=True)
    forward, inverse = dft_tables(length, row_index)
    forward_matrix = forward.reshape(2 * length, 2 * length)
    inverse_matrix = inverse.reshape(2 * length, 2 * length)
    matrix = slab_rows.reshape(2 * length, mode_count * comp_count)
    spectrum = jnp.dot(forward_matrix, matrix, precision=lax.Precision.HIGHEST)
    spectrum = spectrum.reshape(2, length * mode_count, comp_count)
    deriv_rows = derivatives.reshape(length * mode_count, deriv_count)
    taylor_k = contract_rows(deriv_rows, spectrum, comp_count)
    taylor_k = taylor_k.reshape(2 * length, mode_count * comp_count)
    returned = jnp.dot(inverse_matrix, taylor_k, precision=lax.Precision.HIGHEST)
    returned = returned.reshape(2, length, mode_count * comp_count)
    result = lax.all_to_all(returned, ("grp", "dev"), split_axis=1, concat_axis=2, tiled=True)
    return result


def on_device(multipoles, derivatives):
    return convolve_group(multipoles, derivatives)


def solution(mesh):
    in_specs = (P(None, ("grp", "dev"), None), P(None, ("grp", "dev"), None))
    out_specs = P(None, ("grp", "dev"), None)
    return jax.shard_map(
        on_device, mesh=mesh, in_specs=in_specs, out_specs=out_specs, check_vma=False
    )
```

profile of v0, /device:TPU:1, one launch (start us, length us, event | category | flops | bytes accessed | tf_op | source)
XLA Modules:
  0.0 560.5 jit_solution(2674592462002672816)
XLA Ops:
  0.0 40.9 %copy.55 = f32[2,3,41472]{1,0,2:T(2,128)} copy(f32[2,3,41472]{2,0,1:T(2,128)} %param.5) | data formatting | bytes 1990656 | tf_op args[0]
  40.9 48.3 %reshape.123 = f32[128,1,1944]{2,1,0:T(1,128)} reshape(f32[41472,2,3]{2,1,0:T(2,128)} %bitcast.37) | data formatting | bytes 1990656
  89.2 12.3 %all-to-all-start = ((f32[128,1,1944]{2,1,0:T(1,128)}), f32[128,1,1944]{2,1,0:T(1,128)}, u32[]{:S(2)}, u32[]{:S(2)}) async-start(f32[128,1,1944]{2,1,0:T(1,128)} %reshape.123), calls=%async_computation | async-start | bytes 2097152 | tf_op jit(solution)/shard_map/all_to_all | solution.py:82
  101.5 2.3 fusion.16
  103.8 2.4 sine_multiply_fusion
  107.5 1.4 copy.51
  108.9 2.7 copy.53
  113.6 1.8 copy.54
  115.4 1.6 copy.72
  117.7 2.5 copy.59
  120.3 3.1 reshape.118
  123.9 4.3 reduce
  128.3 53.6 %reshape.124 = f32[41472,2,3]{2,1,0:T(2,128)} reshape(f32[128,1944]{1,0:T(8,128)S(1)} %reduce) | data formatting | bytes 1990656
  181.9 38.0 %copy.67 = f32[2,3,128,324]{3,2,0,1:T(8,128)S(1)} copy(f32[2,3,128,324]{1,0,3,2:T(2,128)} %bitcast.38) | data formatting | bytes 1990656 | tf_op jit(solution)/shard_map/all_to_all | solution.py:82
  219.9 2.0 copy.57
  221.9 1.8 reshape.116
  223.7 6.6 %fusion.18 = f32[768,324]{1,0:T(8,128)} fusion(f32[768,768]{1,0:T(8,128)} %bitcast.39, f32[768,324]{1,0:T(8,128)S(1)} %reshape.116), kind=kOutput, calls=%fused_computation.30 | convolution fusion | flops 2293235712 | bytes 4349952 | tf_op jit(solution)/shard_map/dot_general | solution.py:87
  230.3 2.6 reshape.117
  234.2 285.8 %while.14 = (s32[]{:T(128)}, f32[2,1536,81]{2,1,0:T(8,128)}, f32[2,1536,81]{2,1,0:T(8,128)}, f32[1536,289]{1,0:T(8,128)S(1)}, s32[]{:T(128)}, /*index=5*/s32[]{:T(128)}, s32[]{:T(128)}, s32[]{:T(128)}, f32[289,6561]{1,0:T(8,128)}) while((s32[]{:T(128)}, f32[2,1536,81]{2,1,0:T(8,128)}, f32[2,1536,81]{2,1,0:T(8,128)}, ...), condition=%wide.region_1.2_spmd.clone, body=%wide.region_0.1_spmd.sunk.clone.sunk | while | flops 17595656192 | bytes 141222864 | solution.py:70
  234.3 37.5 %fusion.32 = f32[768,6561]{0,1:T(8,128)} fusion(f32[289,6561]{1,0:T(8,128)} %get-tuple-element.202, f32[1536,289]{1,0:T(8,128)S(1)} %get-tuple-element.197, s32[]{:T(128)S(6)} %select_n.65), kind=kOutput, calls=%fused_computation.1.clone.1 | convolution fusion | flops 17474723840 | bytes 28919560 | tf_op jit(solution)/shard_map/while/body/eval_jaxpr/dot_general | solution.py:62
  271.8 17.5 %reshape.126 = f32[768,81,81]{0,2,1:T(8,128)} reshape(f32[768,6561]{0,1:T(8,128)} %fusion.32) | data formatting | bytes 40310784 | tf_op jit(solution)/shard_map/while/body/eval_jaxpr/reshape | solution.py:63
  289.3 27.8 %copy.81 = f32[768,81,81]{2,1,0:T(8,128)} copy(f32[768,81,81]{0,2,1:T(8,128)} %reshape.126) | data formatting | bytes 40310784 | tf_op jit(solution)/shard_map/while/body/eval_jaxpr/reshape | solution.py:63
  318.3 57.5 %convolution_bitcast_fusion.2 = f32[2,768,81]{2,0,1:T(2,128)S(1)} fusion(f32[768,81,81]{2,1,0:T(8,128)} %copy.81, f32[2,768,81]{2,1,0:T(8,128)S(1)} %constant_dynamic-slice_fusion.2), kind=kOutput, calls=%fused_computation.clone.1 | convolution fusion | flops 120932352 | bytes 21150720 | tf_op jit(solution)/shard_map/while/body/eval_jaxpr/pab,rpb->rpa/dot_general | solution.py:65
  377.1 37.4 %fusion.32 = f32[768,6561]{0,1:T(8,128)} fusion(f32[289,6561]{1,0:T(8,128)} %get-tuple-element.202, f32[1536,289]{1,0:T(8,128)S(1)} %get-tuple-element.197, s32[]{:T(128)S(6)} %select_n.65), kind=kOutput, calls=%fused_computation.1.clone.1 | convolution fusion | flops 17474723840 | bytes 28919560 | tf_op jit(solution)/shard_map/while/body/eval_jaxpr/dot_general | solution.py:62
  414.5 17.5 %reshape.126 = f32[768,81,81]{0,2,1:T(8,128)} reshape(f32[768,6561]{0,1:T(8,128)} %fusion.32) | data formatting | bytes 40310784 | tf_op jit(solution)/shard_map/while/body/eval_jaxpr/reshape | solution.py:63
  432.0 27.8 %copy.81 = f32[768,81,81]{2,1,0:T(8,128)} copy(f32[768,81,81]{0,2,1:T(8,128)} %reshape.126) | data formatting | bytes 40310784 | tf_op jit(solution)/shard_map/while/body/eval_jaxpr/reshape | solution.py:63
  461.0 57.5 %convolution_bitcast_fusion.2 = f32[2,768,81]{2,0,1:T(2,128)S(1)} fusion(f32[768,81,81]{2,1,0:T(8,128)} %copy.81, f32[2,768,81]{2,1,0:T(8,128)S(1)} %constant_dynamic-slice_fusion.2), kind=kOutput, calls=%fused_computation.clone.1 | convolution fusion | flops 120932352 | bytes 21150720 | tf_op jit(solution)/shard_map/while/body/eval_jaxpr/pab,rpb->rpa/dot_general | solution.py:65
  520.0 2.0 reshape.119
  522.1 3.7 fusion.4
  525.8 2.4 copy.63
  528.2 29.6 %all_to_all.33 = f32[2,384,324]{2,0,1:T(2,128)S(1)} all-to-all(f32[2,384,324]{2,0,1:T(2,128)S(1)} %copy.63), channel_id=1, replica_groups=mesh['grp'=2,'dev'=64] {'grp','dev'}, dimensions={1} | all-to-all | bytes 1990656 | tf_op jit(solution)/shard_map/all_to_all | solution.py:94
  557.9 2.4 all_to_all.30
  (28 shorter events, 10.9 us)
Async XLA Ops:
  89.2 34.2 %all-to-all-start = ((f32[128,1,1944]{2,1,0:T(1,128)}), f32[128,1,1944]{2,1,0:T(1,128)}, u32[]{:S(2)}, u32[]{:S(2)}) async-start(f32[128,1,1944]{2,1,0:T(1,128)} %reshape.123), calls=%async_computation | async-start | bytes 2097152 | tf_op jit(solution)/shard_map/all_to_all | solution.py:82
  112.0 1.4 copy-start.2
  115.4 2.3 copy-start.5
  318.2 57.6 %copy-start = (f32[2,1536,81]{2,1,0:T(8,128)S(1)}, f32[2,1536,81]{2,1,0:T(8,128)}, u32[]{:S(2)}) copy-start(f32[2,1536,81]{2,1,0:T(8,128)} %get-tuple-element.186) | copy-start | bytes 2985988 | tf_op jit(solution)/shard_map/while
  375.9 1.2 copy-start.1
  461.0 57.6 %copy-start = (f32[2,1536,81]{2,1,0:T(8,128)S(1)}, f32[2,1536,81]{2,1,0:T(8,128)}, u32[]{:S(2)}) copy-start(f32[2,1536,81]{2,1,0:T(8,128)} %get-tuple-element.186) | copy-start | bytes 2985988 | tf_op jit(solution)/shard_map/while
  518.6 1.2 copy-start.1
  520.0 2.0 copy-start.3
  520.0 2.1 copy-start.4
where the time goes:
time: 570 us; the launch traced here: 560 us
  local copies, waits for them, and re-layouts  307 us (54%)
  matrix products  200 us (35%)
  blocking collectives  29.6 us (5%)
  starting transfers between devices  12.3 us (2%)
  other arithmetic  10.5 us (2%)
    unnamed x13, local copies, waits for them, and re-layouts  148 us
    dot_general x2, matrix products, step(): jnp.einsum('pab,rpb->rpa', coupling, moment_block, precision=lax.Precisio...  115 us
    reshape x4, local copies, waits for them, and re-layouts, step(): coupling = coupling.reshape(width, comp_count, comp_count)  90.5 us
    dot_general x2, matrix products, step(): coupling = jnp.dot(deriv_block, table, precision=lax.Precision.HIGHEST)  74.9 us
    all_to_all x3, local copies, waits for them, and re-layouts, convolve_group(): lax.all_to_all(multipoles, ('grp', 'dev'), split_axis=2, concat_axis=1, t...  40.6 us
    all_to_all x1, blocking collectives, convolve_group(): lax.all_to_all(returned, ('grp', 'dev'), split_axis=1, concat_axis=2, til...  29.6 us
    all_to_all x1, starting transfers between devices, convolve_group(): lax.all_to_all(multipoles, ('grp', 'dev'), split_axis=2, concat_axis=1, t...  12.3 us
  transfers between devices with their start and end apart: 1, of which 0 were waited for; matrix products, arithmetic and copies ran while one was open for 4% of the time, Pallas kernels for 0%

commit v1 on v0

v1 whole, which is shorter than its diff:
```python
import functools
import math

import jax
import jax.numpy as jnp
import ml_dtypes
import numpy as np
from jax import lax
from jax.experimental import pallas as pl
from jax.experimental.pallas import tpu as pltpu
from jax.sharding import PartitionSpec as P

ORDER = 8
MESH = pl.DeviceIdType.MESH
F32 = jnp.float32
BF16 = jnp.bfloat16

COMP = 81
NDEV = 128
INNER = 64
NZ = 384
ZL = 3
COLS = 324
HALF = 162
REST = 34
ZROWS = 648
LEAD = 8
PLANE_ROWS = LEAD + ZL * ZROWS + 16
QS = 82
NX = 409


def reduced_terms(highest):
    listed = []
    for total in range(highest + 1):
        for upper in range(min(total, 1) + 1):
            for first in range(total - upper, -1, -1):
                listed.append((first, total - upper - first, upper))
    return listed


LOWER = {t: n for n, t in enumerate(reduced_terms(ORDER))}
HIGHER = {t: n for n, t in enumerate(reduced_terms(2 * ORDER))}


def extended_index():
    place, parts = {}, []
    for total in range(2 * ORDER - 1):
        for first in range(total, -1, -1):
            second = total - first
            place[first, second] = 289 + len(parts)
            parts.append((HIGHER[first + 2, second, 0], HIGHER[first, second + 2, 0]))
    return place, parts


SECOND, SECOND_PARTS = extended_index()


def deriv_place(i, j, c):
    return HIGHER[i, j, c] if c <= 1 else SECOND[i, j]


def dft_table():
    z = (3 * np.arange(NDEV)[None, :] + np.arange(ZL)[:, None]).reshape(-1)
    k = np.arange(NZ)
    angle = 2.0 * np.pi / NZ * (z[:, None] * k[None, :] % NZ)
    c, s = np.cos(angle) / math.sqrt(NZ), np.sin(angle) / math.sqrt(NZ)
    w = np.block([[c, -s], [s, c]])
    high = w.astype(ml_dtypes.bfloat16)
    low = (w - high.astype(np.float64)).astype(ml_dtypes.bfloat16)
    return high, low


def split(x):
    high = x.astype(BF16)
    return high, (x - high.astype(F32)).astype(BF16)


def iotas():
    lane = lax.broadcasted_iota(jnp.int32, (8, 128), 1)
    row = lax.broadcasted_iota(jnp.int32, (8, 128), 0)
    return lane, row


def column_start(owner, h):
    start = COLS * owner + HALF * h
    return start // 128, start % 128


def pack(plane, msg, h, d):
    lane, row = iotas()
    tile, off = column_start(d, h)
    here = lane >= off
    rel = jnp.where(here, lane - off, lane - off + 128)
    main = rest = None
    for z in range(ZL):
        at = LEAD + z * ZROWS + 2 * tile - 2 * z
        v = jnp.where(here, plane[pl.ds(at, 8), :], plane[pl.ds(at + 2, 8), :])
        main = v if z == 0 else jnp.where(row >= 2 * z, v, main)
        at = LEAD + z * ZROWS + 2 * tile - 4
        v = jnp.where(here, plane[pl.ds(at, 8), :], plane[pl.ds(at + 2, 8), :])
        if z:
            v = pltpu.roll(v, REST * z, 1)
        rest = v if z == 0 else jnp.where(rel >= REST * z, v, rest)
    msg[h, pl.ds(pl.multiple_of(8 * d, 8), 8), :] = jnp.where(row >= 6, rest, main)


def unpack(got, plane, h, s):
    lane, row = iotas()
    tile, off = column_start(s, h)
    here = lane >= off
    rel = jnp.where(here, lane - off, lane - off + 128)
    m = got[h, pl.ds(pl.multiple_of(8 * s, 8), 8), :]
    for z in range(ZL):
        mine = (row >= 2 * z) & (row < 2 * z + 2)
        at = LEAD + z * ZROWS + 2 * tile - 2 * z
        pltpu.store(plane.at[pl.ds(at, 8), :], m, mask=mine & here)
        pltpu.store(plane.at[pl.ds(at + 2, 8), :], m, mask=mine & ~here)
        v = pltpu.roll(m, 128 - REST * z, 1) if z else m
        mine = (row >= 6) & (rel < REST)
        at = LEAD + z * ZROWS + 2 * tile - 4
        pltpu.store(plane.at[pl.ds(at, 8), :], v, mask=mine & here)
        pltpu.store(plane.at[pl.ds(at + 2, 8), :], v, mask=mine & ~here)


def send_all(me, msg, got, send_sem, recv_sem, h):
    @pl.loop(1, NDEV)
    def _(i):
        d = (me + i) % NDEV
        pltpu.make_async_remote_copy(
            src_ref=msg.at[h, pl.ds(pl.multiple_of(8 * d, 8), 8), :],
            dst_ref=got.at[h, pl.ds(pl.multiple_of(8 * me, 8), 8), :],
            send_sem=send_sem.at[h],
            recv_sem=recv_sem.at[h],
            device_id=(d // INNER, d % INNER),
            device_id_type=MESH,
        ).start()


def own_copy(me, msg, got, sem, h):
    mine = pl.ds(pl.multiple_of(8 * me, 8), 8)
    return pltpu.make_async_copy(msg.at[h, mine, :], got.at[h, mine, :], sem.at[h])


def wait_bytes(buf, sem, h):
    part = buf.at[h, pl.ds(0, 8 * (NDEV - 1)), :]
    pltpu.make_async_copy(part, part, sem.at[h]).wait()


def prepare(deriv, table):
    @pl.loop(0, 289)
    def _(n):
        for kc in range(3):
            v = deriv[n, :, pl.ds(128 * kc, 128)]
            table[kc, n] = jnp.concatenate([v, v], axis=0)

    @pl.loop(0, 3)
    def _(kc):
        for n, (one, two) in enumerate(SECOND_PARTS):
            table[kc, 289 + n] = -(table[kc, one] + table[kc, two])


def gather_columns(got, xbuf, h, off):
    back = (128 - off) % 128
    base = 2 * h * QS
    for r in range(2):
        for z in range(ZL):
            v = got[h, pl.ds(2 * z + r, NDEV, stride=8), :]
            v = pltpu.roll(v, back, 1).T
            xbuf[r * ZL + z, base : base + 81, :] = v[:81]
            xbuf[r * ZL + z, base + QS : base + QS + 47, :] = v[81:]
        v = pltpu.roll(got[h, pl.ds(6 + r, NDEV, stride=8), :], back, 1).T
        for z in range(ZL):
            at = base + QS + 47
            xbuf[r * ZL + z, at : at + REST, :] = v[REST * z : REST * z + REST]


def forward(xbuf, whigh, wlow, sbuf):
    x = jnp.concatenate([xbuf[n] for n in range(6)], axis=1)
    high, low = split(x)
    dot = functools.partial(jnp.dot, preferred_element_type=F32)
    out = dot(high, whigh[...]) + dot(low, whigh[...]) + dot(high, wlow[...])
    for r in range(2):
        for kc in range(3):
            at = r * NZ + kc * 128
            sbuf[kc, r * 4 * QS : (r + 1) * 4 * QS, :] = out[:, at : at + 128]


def contract(table, sbuf, stage, tbuf):
    @pl.loop(0, 3)
    def _(kc):
        for b in range(COMP):
            stage[b] = sbuf[kc, pl.ds(b, 8, stride=QS), :]
        for c in range(2):
            for i in range(ORDER + 1 - c):
                rows = ORDER + 1 - c - i
                acc = [None] * rows
                for c2 in range(2):
                    for i2 in range(ORDER + 1 - c2):
                        terms = ORDER + 1 - c2 - i2
                        seen = {}
                        for j2 in range(terms):
                            s = stage[LOWER[i2, j2, c2]]
                            for j in range(rows):
                                if j + j2 not in seen:
                                    place = deriv_place(i + i2, j + j2, c + c2)
                                    seen[j + j2] = table[kc, place]
                                v = seen[j + j2] * s
                                acc[j] = v if acc[j] is None else acc[j] + v
                for j in range(rows):
                    tbuf[kc, pl.ds(LOWER[i, j, c], 8, stride=COMP), :] = acc[j]


def backward(tbuf, tarr, whigh, wlow, ybuf):
    for r in range(2):
        for kc in range(3):
            n, at = r * 3 + kc, r * COLS
            tarr[n, 0:128, :] = tbuf[kc, at : at + 128, :]
            tarr[n, 128:256, :] = tbuf[kc, at + HALF : at + HALF + 128, :]
            tarr[n, 256 : 256 + REST, :] = tbuf[kc, at + 128 : at + HALF, :]
            tarr[n, 256 + REST : 256 + 2 * REST, :] = tbuf[kc, at + HALF + 128 : at + COLS, :]
            tarr[n, 256 + 2 * REST :, :] = jnp.zeros((128 - 2 * REST, 128), F32)
    t = jnp.concatenate([tarr[n] for n in range(6)], axis=1)
    high, low = split(t)
    dims = (((1,), (1,)), ((), ()))
    dot = functools.partial(lax.dot_general, dimension_numbers=dims, preferred_element_type=F32)
    ybuf[...] = dot(whigh[...], high) + dot(whigh[...], low) + dot(wlow[...], high)


def scatter_columns(ybuf, msg, h, off):
    lane = lax.broadcasted_iota(jnp.int32, (NDEV, 128), 1)
    rel = jnp.where(lane >= off, lane - off, lane - off + 128)
    for r in range(2):
        rest = None
        for z in range(ZL):
            at = (r * ZL + z) * NDEV
            v = ybuf[at : at + NDEV, 128 * h : 128 * h + 128]
            msg[h, pl.ds(2 * z + r, NDEV, stride=8), :] = pltpu.roll(v, off, 1)
            shift = (off + REST * z + 128 - REST * h) % 128
            v = pltpu.roll(ybuf[at : at + NDEV, 256:384], shift, 1)
            rest = v if z == 0 else jnp.where(rel >= REST * z, v, rest)
        msg[h, pl.ds(6 + r, NDEV, stride=8), :] = rest


def kernel(
    planes_hbm, deriv_hbm, whigh_hbm, wlow_hbm, out_hbm,
    plane, outp, deriv, whigh, wlow, table, msg, got, msg2, got2, xbuf, sbuf, stage, tbuf, tarr, ybuf,
    load_sem, own_sem, send_sem, recv_sem, own_sem2, send_sem2, recv_sem2,
):
    me = lax.axis_index("grp") * INNER + lax.axis_index("dev")
    loads = [
        pltpu.make_async_copy(planes_hbm, plane.at[pl.ds(LEAD, ZL * ZROWS), :], load_sem.at[0]),
        pltpu.make_async_copy(deriv_hbm, deriv, load_sem.at[1]),
        pltpu.make_async_copy(whigh_hbm, whigh, load_sem.at[2]),
        pltpu.make_async_copy(wlow_hbm, wlow, load_sem.at[3]),
    ]
    for copy in loads:
        copy.start()
    barrier = pltpu.get_barrier_semaphore()

    @pl.loop(1, NDEV)
    def _(i):
        d = (me + i) % NDEV
        pl.semaphore_signal(barrier, inc=1, device_id=(d // INNER, d % INNER), device_id_type=MESH)

    plane[0:LEAD, :] = jnp.zeros((LEAD, 128), F32)
    plane[LEAD + ZL * ZROWS :, :] = jnp.zeros((16, 128), F32)
    loads[0].wait()
    for h in range(2):

        @pl.loop(0, NDEV, unroll=4)
        def _(d):
            pack(plane, msg, h, d)

    pl.semaphore_wait(barrier, NDEV - 1)
    for h in range(2):
        send_all(me, msg, got, send_sem, recv_sem, h)
        own_copy(me, msg, got, own_sem, h).start()
    for copy in loads[1:]:
        copy.wait()
    prepare(deriv, table)
    for h in range(2):
        own_copy(me, msg, got, own_sem, h).wait()
        wait_bytes(got, recv_sem, h)
        gather_columns(got, xbuf, h, column_start(me, h)[1])
    forward(xbuf, whigh, wlow, sbuf)
    contract(table, sbuf, stage, tbuf)
    backward(tbuf, tarr, whigh, wlow, ybuf)
    for h in range(2):
        scatter_columns(ybuf, msg2, h, column_start(me, h)[1])
        send_all(me, msg2, got2, send_sem2, recv_sem2, h)
        own_copy(me, msg2, got2, own_sem2, h).start()
    for h in range(2):
        own_copy(me, msg2, got2, own_sem2, h).wait()
        wait_bytes(got2, recv_sem2, h)

        @pl.loop(0, NDEV, unroll=4)
        def _(s):
            unpack(got2, outp, h, s)

    store = pltpu.make_async_copy(outp.at[pl.ds(LEAD, ZL * ZROWS), :], out_hbm, load_sem.at[0])
    store.start()
    for h in range(2):
        wait_bytes(msg, send_sem, h)
        wait_bytes(msg2, send_sem2, h)
    store.wait()


def on_device(multipoles, derivatives):
    planes = jnp.transpose(multipoles, (1, 0, 2)).reshape(ZL, 2, COLS, 128)
    planes = jnp.transpose(planes, (0, 2, 1, 3)).reshape(ZL * ZROWS, 128)
    deriv = jnp.transpose(derivatives, (2, 1, 0))
    high, low = dft_table()
    vmem, dma = pltpu.VMEM, pltpu.SemaphoreType.DMA
    out = pl.pallas_call(
        kernel,
        out_shape=jax.ShapeDtypeStruct((ZL * ZROWS, 128), F32),
        in_specs=[pl.BlockSpec(memory_space=pl.ANY)] * 4,
        out_specs=pl.BlockSpec(memory_space=pl.ANY),
        scratch_shapes=[
            vmem((PLANE_ROWS, 128), F32),
            vmem((PLANE_ROWS, 128), F32),
            vmem((289, 4, NZ), F32),
            vmem((2 * NZ, 2 * NZ), BF16),
            vmem((2 * NZ, 2 * NZ), BF16),
            vmem((3, NX, 8, 128), F32),
            vmem((2, 8 * NDEV, 128), F32),
            vmem((2, 8 * NDEV, 128), F32),
            vmem((2, 8 * NDEV, 128), F32),
            vmem((2, 8 * NDEV, 128), F32),
            vmem((6, 4 * QS, 128), F32),
            vmem((3, 8 * QS, 128), F32),
            vmem((COMP, 8, 128), F32),
            vmem((3, 8 * COMP, 128), F32),
            vmem((6, 384, 128), F32),
            vmem((2 * NZ, 384), F32),
            dma((4,)), dma((2,)), dma((2,)), dma((2,)), dma((2,)), dma((2,)), dma((2,)),
        ],
        compiler_params=pltpu.CompilerParams(
            collective_id=0, has_side_effects=True, vmem_limit_bytes=60 * 1024 * 1024
        ),
        name="m2l",
    )(planes, deriv, jnp.asarray(high), jnp.asarray(low))
    out = jnp.transpose(out.reshape(ZL, COLS, 2, 128), (0, 2, 1, 3)).reshape(ZL, 2, COLS * 128)
    return jnp.transpose(out, (1, 0, 2))


def solution(mesh):
    in_specs = (P(None, ("grp", "dev"), None), P(None, ("grp", "dev"), None))
    out_specs = P(None, ("grp", "dev"), None)
    return jax.shard_map(
        on_device, mesh=mesh, in_specs=in_specs, out_specs=out_specs, check_vma=False
    )
```

time: 570 us -> 69.3 us (0.12); the launches traced: 560 us -> 69.2 us
  local copies, waits for them, and re-layouts: 307 us -> 5.68 us
  matrix products: 200 us -> 0 us
  Pallas kernels: 0 us -> 63.5 us
  blocking collectives: 29.6 us -> 0 us
  starting transfers between devices: 12.3 us -> 0 us
  other arithmetic: 10.5 us -> 0 us
    dot_general x6 -> x0, matrix products: 200 us -> none  [the longest x2 115 us: step(): jnp.einsum('pab,rpb->rpa', coupling, moment_block, precision=lax.Precisio...]
    unnamed x13 -> x1, local copies, waits for them, and re-layouts: 148 us -> 2.22 us
    reshape x8 -> x1, local copies, waits for them, and re-layouts: 100 us -> 2 us  [on_device(): planes = jnp.transpose(multipoles, (1, 0, 2)).reshape(ZL, 2, COLS, 128)]
    pallas_call x0 -> x1, Pallas kernels: none -> 63.5 us  [on_device(): pl.pallas_call(kernel, out_shape=jax.ShapeDtypeStruct((ZL * ZROWS, 128),...]
    all_to_all x5 -> x0, local copies, waits for them, and re-layouts: 43.1 us -> none  [the longest x3 40.6 us: convolve_group(): lax.all_to_all(multipoles, ('grp', 'dev'), split_axis=2, concat_axis=1, t...]
    all_to_all x1 -> x0, blocking collectives: 29.6 us -> none  [convolve_group(): lax.all_to_all(returned, ('grp', 'dev'), split_axis=1, concat_axis=2, til...]
    all_to_all x1 -> x0, starting transfers between devices: 12.3 us -> none  [convolve_group(): lax.all_to_all(multipoles, ('grp', 'dev'), split_axis=2, concat_axis=1, t...]
    another operation x5 -> x0, local copies, waits for them, and re-layouts: 7.68 us -> none  [the longest x2 4.09 us: dft_tables(): jnp.stack([jnp.stack([cosine.T, -sine.T], 1), jnp.stack([sine.T, cosine.T...]
  transfers between devices with their start and end apart: 1 -> 0, of which waited for: 0 -> 0; matrix products, arithmetic and copies ran while one was open for 4% -> 0% of each run, Pallas kernels for 0% -> 0%
where the time goes in v1:
time: 69.3 us; the launch traced here: 69.2 us
  Pallas kernels  63.5 us (92%)
  local copies, waits for them, and re-layouts  5.68 us (8%)
    pallas_call x1, Pallas kernels, on_device(): pl.pallas_call(kernel, out_shape=jax.ShapeDtypeStruct((ZL * ZROWS, 128),...  63.5 us
    unnamed x1, local copies, waits for them, and re-layouts  2.22 us
    reshape x1, local copies, waits for them, and re-layouts, on_device(): planes = jnp.transpose(multipoles, (1, 0, 2)).reshape(ZL, 2, COLS, 128)  2 us
    transpose x1, local copies, waits for them, and re-layouts, on_device(): planes = jnp.transpose(planes, (0, 2, 1, 3)).reshape(ZL * ZROWS, 128)  1.46 us

profile of v1, /device:TPU:1, one launch (start us, length us, event | category | flops | bytes accessed | tf_op | source)
XLA Modules:
  0.0 69.2 jit_solution(15979877520292365591)
XLA Ops:
  0.0 2.0 %reshape.12 = f32[3,2,324,128]{3,2,1,0:T(8,128)S(1)} reshape(f32[3,2,41472]{2,1,0:T(2,128)} %bitcast.15) | data formatting | bytes 1990656 | tf_op jit(solution)/shard_map/reshape | solution.py:310
  2.0 1.5 %copy.6 = f32[3,324,2,128]{3,2,1,0:T(2,128)} copy(f32[3,324,2,128]{3,1,2,0:T(8,128)S(1)} %bitcast.11) | data formatting | bytes 1990656 | tf_op jit(solution)/shard_map/transpose | solution.py:311
  3.5 63.5 %m2l.1 = f32[1944,128]{1,0:T(8,128)} custom-call(f32[1944,128]{1,0:T(8,128)} %bitcast.12, f32[289,4,384]{2,1,0:T(4,128)} %bitcast.14, bf16[768,768]{1,0:T(8,128)(2,1)} %constant.4.clone.whigh_hbm, bf16[768,768]{1,0:T(8,128)(2,1)} %constant.5.clone.wlow_hbm), custom_call_target="tpu_custom_call" | custom-call | tf_op jit(solution)/shard_map/m2l/pallas_call | solution.py:315
  66.9 2.2 %copy.8 = f32[2,3,41472]{2,0,1:T(2,128)} copy(f32[2,3,41472]{2,0,1:T(2,128)} %bitcast.13) | data formatting | bytes 1990656

commit v2 on v1

--- a/solution.py
+++ b/solution.py
@@ -7,6 +7,7 @@
 import numpy as np
 from jax import lax
 from jax.experimental import pallas as pl
+from jax.experimental.layout import Layout, with_layout_constraint
 from jax.experimental.pallas import tpu as pltpu
 from jax.sharding import PartitionSpec as P
 
@@ -27,7 +28,7 @@
 LEAD = 8
 PLANE_ROWS = LEAD + ZL * ZROWS + 16
 QS = 82
-NX = 409
+MROWS = 168
 
 
 def reduced_terms(highest):
@@ -43,21 +44,54 @@
 HIGHER = {t: n for n, t in enumerate(reduced_terms(2 * ORDER))}
 
 
-def extended_index():
-    place, parts = {}, []
-    for total in range(2 * ORDER - 1):
-        for first in range(total, -1, -1):
-            second = total - first
-            place[first, second] = 289 + len(parts)
-            parts.append((HIGHER[first + 2, second, 0], HIGHER[first, second + 2, 0]))
-    return place, parts
-
-
-SECOND, SECOND_PARTS = extended_index()
-
-
-def deriv_place(i, j, c):
-    return HIGHER[i, j, c] if c <= 1 else SECOND[i, j]
+class Plan:
+    def __init__(self):
+        self.count = len(HIGHER)
+        self.second, self.level1, self.level2 = [], [], []
+        self.pairs = []
+        self.one = {}
+        top = 2 * ORDER
+        for total in range(top + 1):
+            for i in range(total + 1):
+                j = total - i
+                d0, d1 = HIGHER[i, j, 0], HIGHER.get((i, j, 1))
+                self.one["p", i, j] = d1
+                self.one["a", i, j] = d0
+                if d1 is not None:
+                    self.one["a", i, j] = self.fresh()
+                    self.level1.append((self.one["a", i, j], d0, d1))
+                self.one["b", i, j] = None
+                if total <= top - 2:
+                    self.one["b", i, j] = self.fresh()
+                    self.second.append((self.one["b", i, j], HIGHER[i + 2, j, 0], HIGHER[i, j + 2, 0], d1))
+        for total in range(top + 1):
+            for i in range(total + 1):
+                for kind in "pab":
+                    own, other = self.one[kind, i, total - i], self.one.get((kind, i + 1, total - i))
+                    if own is not None:
+                        self.pairs.append((own, other))
+        self.two = {}
+        for kind in "pab":
+            for i in range(top + 1):
+                for m in range(ORDER + 1):
+                    even, odd, after = (self.one.get((kind, i, 2 * m + e)) for e in range(3))
+                    self.two[kind, "p", i, m] = odd
+                    self.two[kind, "a", i, m] = self.minus(even, odd)
+                    self.two[kind, "b", i, m] = self.minus(after, odd)
+
+    def fresh(self):
+        self.count += 1
+        return self.count - 1
+
+    def minus(self, x, y):
+        if y is None:
+            return x
+        slot = self.fresh()
+        self.level2.append((slot, x, y))
+        return slot
+
+
+PLAN = Plan()
 
 
 def dft_table():
@@ -147,32 +181,49 @@
     pltpu.make_async_copy(part, part, sem.at[h]).wait()
 
 
-def prepare(deriv, table):
-    @pl.loop(0, 289)
+def prepare_base(deriv, table):
+    @pl.loop(0, len(HIGHER))
     def _(n):
-        for kc in range(3):
-            v = deriv[n, :, pl.ds(128 * kc, 128)]
-            table[kc, n] = jnp.concatenate([v, v], axis=0)
-
-    @pl.loop(0, 3)
-    def _(kc):
-        for n, (one, two) in enumerate(SECOND_PARTS):
-            table[kc, 289 + n] = -(table[kc, one] + table[kc, two])
+        v = [deriv[n, :, pl.ds(128 * kc, 128)] for kc in range(3)]
+        for h in range(2):
+            v0, v1, v2 = (x[2 * h : 2 * h + 2] for x in v)
+            table[h, n] = jnp.concatenate([v0, v0, v1, v1], axis=0)
+            table[2 + h, n] = jnp.concatenate([v2, v2, v2, v2], axis=0)
+
+
+def prepare_tables(table):
+    row = lax.broadcasted_iota(jnp.int32, (8, 128), 0)
+
+    @pl.loop(0, 4)
+    def _(n):
+        for slot, x, y in PLAN.level1:
+            table[n, slot] = table[n, x] - table[n, y]
+        for slot, x, y, z in PLAN.second:
+            table[n, slot] = -(table[n, x] + table[n, y]) - table[n, z]
+
+    @pl.loop(2, 4)
+    def _(n):
+        for own, other in PLAN.pairs:
+            up = jnp.zeros((8, 128), F32) if other is None else table[n, other]
+            table[n, own] = jnp.where(row < 4, table[n, own], up)
+
+    @pl.loop(0, 4)
+    def _(n):
+        for slot, x, y in PLAN.level2:
+            table[n, slot] = -table[n, y] if x is None else table[n, x] - table[n, y]
 
 
 def gather_columns(got, xbuf, h, off):
     back = (128 - off) % 128
-    base = 2 * h * QS
     for r in range(2):
         for z in range(ZL):
             v = got[h, pl.ds(2 * z + r, NDEV, stride=8), :]
             v = pltpu.roll(v, back, 1).T
-            xbuf[r * ZL + z, base : base + 81, :] = v[:81]
-            xbuf[r * ZL + z, base + QS : base + QS + 47, :] = v[81:]
+            xbuf[r * ZL + z, 0:81, :] = v[:81]
+            xbuf[r * ZL + z, QS : QS + 47, :] = v[81:]
         v = pltpu.roll(got[h, pl.ds(6 + r, NDEV, stride=8), :], back, 1).T
         for z in range(ZL):
-            at = base + QS + 47
-            xbuf[r * ZL + z, at : at + REST, :] = v[REST * z : REST * z + REST]
+            xbuf[r * ZL + z, QS + 47 : QS + 47 + REST, :] = v[REST * z : REST * z + REST]
 
 
 def forward(xbuf, whigh, wlow, sbuf):
@@ -182,69 +233,123 @@
     out = dot(high, whigh[...]) + dot(low, whigh[...]) + dot(high, wlow[...])
     for r in range(2):
         for kc in range(3):
-            at = r * NZ + kc * 128
-            sbuf[kc, r * 4 * QS : (r + 1) * 4 * QS, :] = out[:, at : at + 128]
-
-
-def contract(table, sbuf, stage, tbuf):
-    @pl.loop(0, 3)
-    def _(kc):
-        for b in range(COMP):
-            stage[b] = sbuf[kc, pl.ds(b, 8, stride=QS), :]
-        for c in range(2):
-            for i in range(ORDER + 1 - c):
-                rows = ORDER + 1 - c - i
-                acc = [None] * rows
-                for c2 in range(2):
-                    for i2 in range(ORDER + 1 - c2):
-                        terms = ORDER + 1 - c2 - i2
-                        seen = {}
-                        for j2 in range(terms):
-                            s = stage[LOWER[i2, j2, c2]]
-                            for j in range(rows):
-                                if j + j2 not in seen:
-                                    place = deriv_place(i + i2, j + j2, c + c2)
-                                    seen[j + j2] = table[kc, place]
-                                v = seen[j + j2] * s
-                                acc[j] = v if acc[j] is None else acc[j] + v
-                for j in range(rows):
-                    tbuf[kc, pl.ds(LOWER[i, j, c], 8, stride=COMP), :] = acc[j]
-
-
-def backward(tbuf, tarr, whigh, wlow, ybuf):
+            at, row = r * NZ + kc * 128, (2 * kc + r) * 2 * QS
+            sbuf[row : row + 2 * QS, :] = out[: 2 * QS, at : at + 128]
+
+
+def contract(table, n, stage, paired, finish):
+    step = 2 if paired else 1
+    inputs = {}
+    spare = [COMP]
+
+    def added(x, y):
+        if y is None:
+            return x
+        stage[spare[0]] = stage[x] + stage[y]
+        spare[0] += 1
+        return spare[0] - 1
+
+    part = [{}, {}]
+    for c in range(2):
+        for i in range(0, ORDER + 1 - c, step):
+            for j in range(ORDER + 1 - c - i):
+                part[c][i, j] = LOWER[i, j, c]
+    inputs["a"], inputs["b"] = part
+    inputs["p"] = {x: added(s, part[1].get(x)) for x, s in part[0].items()}
+    leaves = {}
+    for kind in "pab":
+        even = {(i, j // 2): s for (i, j), s in inputs[kind].items() if j % 2 == 0}
+        odd = {(i, j // 2): s for (i, j), s in inputs[kind].items() if j % 2 == 1}
+        leaves[kind] = {"a": even, "b": odd, "p": {x: added(s, odd.get(x)) for x, s in even.items()}}
+
+    def leaf_row(kind, sub, i, rows):
+        acc = [None] * rows
+        seen = {}
+        for (i2, m2), slot in leaves[kind][sub].items():
+            s = stage[slot]
+            for m in range(rows):
+                key = i + i2, m + m2
+                place = PLAN.two.get((kind, sub, *key))
+                if place is None:
+                    continue
+                if key not in seen:
+                    seen[key] = table[n, place]
+                v = seen[key] * s
+                acc[m] = v if acc[m] is None else acc[m] + v
+        return acc
+
+    def row_of(kind, i, count):
+        evens, odds = (count + 1) // 2, count // 2
+        p = leaf_row(kind, "p", i, evens)
+        a = leaf_row(kind, "a", i, evens)
+        b = leaf_row(kind, "b", i, odds) if odds else []
+        out = [None] * count
+        for m in range(evens):
+            out[2 * m] = a[m] if p[m] is None else p[m] + a[m]
+        for m in range(odds):
+            out[2 * m + 1] = p[m] + b[m]
+        return out
+
+    for i in range(ORDER + 1):
+        count = ORDER + 1 - i
+        p = row_of("p", i, count)
+        a = row_of("a", i, count)
+        b = row_of("b", i, count - 1) if count > 1 else []
+        for j in range(count):
+            finish(LOWER[i, j, 0], a[j] if p[j] is None else p[j] + a[j])
+        for j in range(count - 1):
+            finish(LOWER[i, j, 1], p[j] + b[j])
+
+
+def contract_half(table, h, sbuf, stage, stage2, tbuf):
+    row = lax.broadcasted_iota(jnp.int32, (8, 128), 0)
+    for b in range(COMP):
+        stage[b] = sbuf[pl.ds(b, 8, stride=QS), :]
+    for (i, j, c), b in LOWER.items():
+        if i % 2 == 0:
+            v = sbuf[pl.ds(8 * QS + b, 8, stride=QS), :]
+            up = LOWER.get((i + 1, j, c))
+            up = jnp.zeros((8, 128), F32) if up is None else sbuf[pl.ds(4 * QS + up, 8, stride=QS), :]
+            stage2[b] = jnp.where(row < 4, v, up)
+
+    def finish(a, v):
+        tbuf[pl.ds(a, 8, stride=COMP), :] = v
+
+    def finish2(a, v):
+        tbuf[pl.ds(8 * COMP + a, 8, stride=COMP), :] = v + pltpu.roll(v, 4, 0)
+
+    contract(table, h, stage, False, finish)
+    contract(table, 2 + h, stage2, True, finish2)
+
+
+def backward(tbuf, vhigh, vlow, ybuf):
+    t = jnp.concatenate([tbuf[HALF * (2 * kc + r) : HALF * (2 * kc + r) + MROWS, :] for r in range(2) for kc in range(3)], axis=1)
+    high, low = split(t)
+    dot = functools.partial(jnp.dot, preferred_element_type=F32)
+    ybuf[...] = dot(high, vhigh[...]) + dot(low, vhigh[...]) + dot(high, vlow[...])
+
+
+def scatter_columns(ybuf, rest, msg, h, off):
     for r in range(2):
-        for kc in range(3):
-            n, at = r * 3 + kc, r * COLS
-            tarr[n, 0:128, :] = tbuf[kc, at : at + 128, :]
-            tarr[n, 128:256, :] = tbuf[kc, at + HALF : at + HALF + 128, :]
-            tarr[n, 256 : 256 + REST, :] = tbuf[kc, at + 128 : at + HALF, :]
-            tarr[n, 256 + REST : 256 + 2 * REST, :] = tbuf[kc, at + HALF + 128 : at + COLS, :]
-            tarr[n, 256 + 2 * REST :, :] = jnp.zeros((128 - 2 * REST, 128), F32)
-    t = jnp.concatenate([tarr[n] for n in range(6)], axis=1)
-    high, low = split(t)
-    dims = (((1,), (1,)), ((), ()))
-    dot = functools.partial(lax.dot_general, dimension_numbers=dims, preferred_element_type=F32)
-    ybuf[...] = dot(whigh[...], high) + dot(whigh[...], low) + dot(wlow[...], high)
-
-
-def scatter_columns(ybuf, msg, h, off):
-    lane = lax.broadcasted_iota(jnp.int32, (NDEV, 128), 1)
-    rel = jnp.where(lane >= off, lane - off, lane - off + 128)
-    for r in range(2):
-        rest = None
         for z in range(ZL):
             at = (r * ZL + z) * NDEV
-            v = ybuf[at : at + NDEV, 128 * h : 128 * h + 128]
+            v = ybuf[0:128, at : at + NDEV].T
             msg[h, pl.ds(2 * z + r, NDEV, stride=8), :] = pltpu.roll(v, off, 1)
-            shift = (off + REST * z + 128 - REST * h) % 128
-            v = pltpu.roll(ybuf[at : at + NDEV, 256:384], shift, 1)
-            rest = v if z == 0 else jnp.where(rel >= REST * z, v, rest)
-        msg[h, pl.ds(6 + r, NDEV, stride=8), :] = rest
+            rest[r, REST * z : REST * z + REST, :] = ybuf[128:HALF, at : at + NDEV]
+        v = pltpu.roll(rest[r].T, off, 1)
+        msg[h, pl.ds(6 + r, NDEV, stride=8), :] = v
+
+
+def transpose_table(w, v):
+    for x in range(6):
+        for y in range(6):
+            block = w[128 * x : 128 * x + 128, 128 * y : 128 * y + 128].astype(F32)
+            v[128 * y : 128 * y + 128, 128 * x : 128 * x + 128] = block.T.astype(BF16)
 
 
 def kernel(
     planes_hbm, deriv_hbm, whigh_hbm, wlow_hbm, out_hbm,
-    plane, outp, deriv, whigh, wlow, table, msg, got, msg2, got2, xbuf, sbuf, stage, tbuf, tarr, ybuf,
+    plane, outp, deriv, whigh, wlow, vhigh, vlow, table, msg, got, msg2, got2, xbuf, sbuf, stage, stage2, tbuf, ybuf, rest,
     load_sem, own_sem, send_sem, recv_sem, own_sem2, send_sem2, recv_sem2,
 ):
     me = lax.axis_index("grp") * INNER + lax.axis_index("dev")
@@ -266,30 +371,39 @@
     plane[0:LEAD, :] = jnp.zeros((LEAD, 128), F32)
     plane[LEAD + ZL * ZROWS :, :] = jnp.zeros((16, 128), F32)
     loads[0].wait()
+
     for h in range(2):
 
         @pl.loop(0, NDEV, unroll=4)
         def _(d):
             pack(plane, msg, h, d)
 
-    pl.semaphore_wait(barrier, NDEV - 1)
-    for h in range(2):
+        if h == 0:
+            pl.semaphore_wait(barrier, NDEV - 1)
         send_all(me, msg, got, send_sem, recv_sem, h)
         own_copy(me, msg, got, own_sem, h).start()
     for copy in loads[1:]:
         copy.wait()
-    prepare(deriv, table)
-    for h in range(2):
+    prepare_base(deriv, table)
+    prepare_tables(table)
+    transpose_table(whigh, vhigh)
+    transpose_table(wlow, vlow)
+    xbuf[:, 2 * QS :, :] = jnp.zeros((6, MROWS - 2 * QS, 128), F32)
+    rest[:, 3 * REST :, :] = jnp.zeros((2, 128 - 3 * REST, 128), F32)
+
+    @pl.loop(0, 2)
+    def _(h):
+        off = column_start(me, h)[1]
         own_copy(me, msg, got, own_sem, h).wait()
         wait_bytes(got, recv_sem, h)
-        gather_columns(got, xbuf, h, column_start(me, h)[1])
-    forward(xbuf, whigh, wlow, sbuf)
-    contract(table, sbuf, stage, tbuf)
-    backward(tbuf, tarr, whigh, wlow, ybuf)
-    for h in range(2):
-        scatter_columns(ybuf, msg2, h, column_start(me, h)[1])
+        gather_columns(got, xbuf, h, off)
+        forward(xbuf, whigh, wlow, sbuf)
+        contract_half(table, h, sbuf, stage, stage2, tbuf)
+        backward(tbuf, vhigh, vlow, ybuf)
+        scatter_columns(ybuf, rest, msg2, h, off)
         send_all(me, msg2, got2, send_sem2, recv_sem2, h)
         own_copy(me, msg2, got2, own_sem2, h).start()
+
     for h in range(2):
         own_copy(me, msg2, got2, own_sem2, h).wait()
         wait_bytes(got2, recv_sem2, h)
@@ -307,8 +421,8 @@
 
 
 def on_device(multipoles, derivatives):
-    planes = jnp.transpose(multipoles, (1, 0, 2)).reshape(ZL, 2, COLS, 128)
-    planes = jnp.transpose(planes, (0, 2, 1, 3)).reshape(ZL * ZROWS, 128)
+    planes = with_layout_constraint(multipoles.reshape(2, ZL, COLS, 128), Layout((1, 2, 0, 3)))
+    planes = jnp.transpose(planes, (1, 2, 0, 3)).reshape(ZL * ZROWS, 128)
     deriv = jnp.transpose(derivatives, (2, 1, 0))
     high, low = dft_table()
     vmem, dma = pltpu.VMEM, pltpu.SemaphoreType.DMA
@@ -323,17 +437,20 @@
             vmem((289, 4, NZ), F32),
             vmem((2 * NZ, 2 * NZ), BF16),
             vmem((2 * NZ, 2 * NZ), BF16),
-            vmem((3, NX, 8, 128), F32),
+            vmem((2 * NZ, 2 * NZ), BF16),
+            vmem((2 * NZ, 2 * NZ), BF16),
+            vmem((4, PLAN.count, 8, 128), F32),
             vmem((2, 8 * NDEV, 128), F32),
             vmem((2, 8 * NDEV, 128), F32),
             vmem((2, 8 * NDEV, 128), F32),
             vmem((2, 8 * NDEV, 128), F32),
-            vmem((6, 4 * QS, 128), F32),
-            vmem((3, 8 * QS, 128), F32),
-            vmem((COMP, 8, 128), F32),
-            vmem((3, 8 * COMP, 128), F32),
-            vmem((6, 384, 128), F32),
-            vmem((2 * NZ, 384), F32),
+            vmem((6, MROWS, 128), F32),
+            vmem((16 * QS, 128), F32),
+            vmem((3 * COMP, 8, 128), F32),
+            vmem((3 * COMP, 8, 128), F32),
+            vmem((16 * COMP, 128), F32),
+            vmem((MROWS, 2 * NZ), F32),
+            vmem((2, 128, 128), F32),
             dma((4,)), dma((2,)), dma((2,)), dma((2,)), dma((2,)), dma((2,)), dma((2,)),
         ],
         compiler_params=pltpu.CompilerParams(

time: 69.3 us -> 55.4 us (0.80)
  Pallas kernels: 63.5 us -> 53 us
  local copies, waits for them, and re-layouts: 5.68 us -> 2.22 us
    pallas_call x1, Pallas kernels: 63.5 us -> 53 us  [on_device(): pl.pallas_call(kernel, out_shape=jax.ShapeDtypeStruct((ZL * ZROWS, 128),...]
    reshape x1 -> x0, local copies, waits for them, and re-layouts: 2 us -> none  [on_device(): planes = jnp.transpose(multipoles, (1, 0, 2)).reshape(ZL, 2, COLS, 128)]
    transpose x1 -> x0, local copies, waits for them, and re-layouts: 1.46 us -> none  [on_device(): planes = jnp.transpose(planes, (0, 2, 1, 3)).reshape(ZL * ZROWS, 128)]
where the time goes in v2:
time: 55.4 us; the launch traced here: 55.2 us
  Pallas kernels  53 us (96%)
  local copies, waits for them, and re-layouts  2.22 us (4%)
    pallas_call x1, Pallas kernels, on_device(): pl.pallas_call(kernel, out_shape=jax.ShapeDtypeStruct((ZL * ZROWS, 128),...  53 us
    unnamed x1, local copies, waits for them, and re-layouts  2.22 us

profile of v2, /device:TPU:1, one launch (start us, length us, event | category | flops | bytes accessed | tf_op | source)
XLA Modules:
  0.0 55.2 jit_solution(730403657227822402)
XLA Ops:
  0.0 53.0 %m2l.1 = f32[1944,128]{1,0:T(8,128)} custom-call(f32[1944,128]{1,0:T(8,128)} %bitcast.15, f32[289,4,384]{2,1,0:T(4,128)} %bitcast.14, bf16[768,768]{1,0:T(8,128)(2,1)} %constant.4.clone.whigh_hbm, bf16[768,768]{1,0:T(8,128)(2,1)} %constant.5.clone.wlow_hbm), custom_call_target="tpu_custom_call" | custom-call | tf_op jit(solution)/shard_map/m2l/pallas_call | solution.py:429
  53.0 2.2 %copy.6 = f32[2,3,41472]{2,0,1:T(2,128)} copy(f32[2,3,41472]{2,0,1:T(2,128)} %bitcast.13) | data formatting | bytes 1990656

commit v3 on v2

--- a/solution.py
+++ b/solution.py
@@ -27,8 +27,6 @@
 ZROWS = 648
 LEAD = 8
 PLANE_ROWS = LEAD + ZL * ZROWS + 16
-QS = 82
-MROWS = 168
 
 
 def reduced_terms(highest):
@@ -118,7 +116,7 @@
 
 def column_start(owner, h):
     start = COLS * owner + HALF * h
-    return start // 128, start % 128
+    return start >> 7, start & 127
 
 
 def pack(plane, msg, h, d):
@@ -143,32 +141,46 @@
     lane, row = iotas()
     tile, off = column_start(s, h)
     here = lane >= off
-    rel = jnp.where(here, lane - off, lane - off + 128)
+    column = (row >> 1) * 128 + lane - off
+    mask = (column >= 0) & (column < HALF)
+    first, second = row < 2, row < 4
     m = got[h, pl.ds(pl.multiple_of(8 * s, 8), 8), :]
-    for z in range(ZL):
-        mine = (row >= 2 * z) & (row < 2 * z + 2)
-        at = LEAD + z * ZROWS + 2 * tile - 2 * z
-        pltpu.store(plane.at[pl.ds(at, 8), :], m, mask=mine & here)
-        pltpu.store(plane.at[pl.ds(at + 2, 8), :], m, mask=mine & ~here)
-        v = pltpu.roll(m, 128 - REST * z, 1) if z else m
-        mine = (row >= 6) & (rel < REST)
-        at = LEAD + z * ZROWS + 2 * tile - 4
-        pltpu.store(plane.at[pl.ds(at, 8), :], v, mask=mine & here)
-        pltpu.store(plane.at[pl.ds(at + 2, 8), :], v, mask=mine & ~here)
+    down, up, up2 = pltpu.roll(m, 2, 0), pltpu.roll(m, 6, 0), pltpu.roll(m, 4, 0)
+    for z, (top, mid) in enumerate(((m, down), (up, m), (up2, up))):
+        rest, rest2 = up2, up
+        if z:
+            rest, rest2 = pltpu.roll(up2, 128 - REST * z, 1), pltpu.roll(up, 128 - REST * z, 1)
+        v = jnp.where(first, top, jnp.where(second, jnp.where(here, rest, mid), rest2))
+        pltpu.store(plane.at[pl.ds(LEAD + z * ZROWS + 2 * tile, 8), :], v, mask=mask)
+
+
+def each_other(me, action):
+    step = 9
+
+    @pl.loop(0, (NDEV - 2) // step)
+    def _(t):
+        for u in range(step):
+            action((me + step * t + u + 1) & (NDEV - 1))
+
+    action((me + NDEV - 1) & (NDEV - 1))
+
+
+def device(d):
+    return (d >> 6, d & (INNER - 1))
 
 
 def send_all(me, msg, got, send_sem, recv_sem, h):
-    @pl.loop(1, NDEV)
-    def _(i):
-        d = (me + i) % NDEV
+    def send(d):
         pltpu.make_async_remote_copy(
             src_ref=msg.at[h, pl.ds(pl.multiple_of(8 * d, 8), 8), :],
             dst_ref=got.at[h, pl.ds(pl.multiple_of(8 * me, 8), 8), :],
             send_sem=send_sem.at[h],
             recv_sem=recv_sem.at[h],
-            device_id=(d // INNER, d % INNER),
+            device_id=device(d),
             device_id_type=MESH,
         ).start()
+
+    each_other(me, send)
 
 
 def own_copy(me, msg, got, sem, h):
@@ -182,13 +194,15 @@
 
 
 def prepare_base(deriv, table):
-    @pl.loop(0, len(HIGHER))
-    def _(n):
-        v = [deriv[n, :, pl.ds(128 * kc, 128)] for kc in range(3)]
-        for h in range(2):
-            v0, v1, v2 = (x[2 * h : 2 * h + 2] for x in v)
-            table[h, n] = jnp.concatenate([v0, v0, v1, v1], axis=0)
-            table[2 + h, n] = jnp.concatenate([v2, v2, v2, v2], axis=0)
+    @pl.loop(0, 17)
+    def _(t):
+        for u in range(17):
+            n = 17 * t + u
+            v = [deriv[n, :, pl.ds(128 * kc, 128)] for kc in range(3)]
+            for h in range(2):
+                v0, v1, v2 = (x[2 * h : 2 * h + 2] for x in v)
+                table[h, n] = jnp.concatenate([v0, v0, v1, v1], axis=0)
+                table[2 + h, n] = jnp.concatenate([v2, v2, v2, v2], axis=0)
 
 
 def prepare_tables(table):
@@ -213,28 +227,34 @@
             table[n, slot] = -table[n, y] if x is None else table[n, x] - table[n, y]
 
 
-def gather_columns(got, xbuf, h, off):
-    back = (128 - off) % 128
+def put(high, low, n, v, lanes):
+    h, l = split(v)
+    high[128 * n : 128 * n + 128, lanes] = h
+    low[128 * n : 128 * n + 128, lanes] = l
+
+
+def gather_columns(got, xhigh, xlow, h, off):
     for r in range(2):
+        rest = got[h, pl.ds(6 + r, NDEV, stride=8), :]
         for z in range(ZL):
             v = got[h, pl.ds(2 * z + r, NDEV, stride=8), :]
-            v = pltpu.roll(v, back, 1).T
-            xbuf[r * ZL + z, 0:81, :] = v[:81]
-            xbuf[r * ZL + z, QS : QS + 47, :] = v[81:]
-        v = pltpu.roll(got[h, pl.ds(6 + r, NDEV, stride=8), :], back, 1).T
-        for z in range(ZL):
-            xbuf[r * ZL + z, QS + 47 : QS + 47 + REST, :] = v[REST * z : REST * z + REST]
-
-
-def forward(xbuf, whigh, wlow, sbuf):
-    x = jnp.concatenate([xbuf[n] for n in range(6)], axis=1)
-    high, low = split(x)
+            put(xhigh, xlow, r * ZL + z, pltpu.roll(v, (128 - off) & 127, 1), slice(0, 128))
+            v = pltpu.roll(rest, (256 - off - REST * z) & 127, 1)
+            put(xhigh, xlow, r * ZL + z, v, slice(128, 256))
+
+
+def product(whigh, wlow, high, low):
     dot = functools.partial(jnp.dot, preferred_element_type=F32)
-    out = dot(high, whigh[...]) + dot(low, whigh[...]) + dot(high, wlow[...])
+    return dot(whigh[...], high[...]) + dot(whigh[...], low[...]) + dot(wlow[...], high[...])
+
+
+def forward(xhigh, xlow, vhigh, vlow, sbuf):
+    out = product(vhigh, vlow, xhigh, xlow)
     for r in range(2):
         for kc in range(3):
-            at, row = r * NZ + kc * 128, (2 * kc + r) * 2 * QS
-            sbuf[row : row + 2 * QS, :] = out[: 2 * QS, at : at + 128]
+            at, row = 128 * (3 * r + kc), (2 * kc + r) * HALF
+            sbuf[row : row + 128, :] = out[at : at + 128, 0:128].T
+            sbuf[row + 128 : row + HALF, :] = out[at : at + 128, 128:256].T[:REST]
 
 
 def contract(table, n, stage, paired, finish):
@@ -262,54 +282,66 @@
         odd = {(i, j // 2): s for (i, j), s in inputs[kind].items() if j % 2 == 1}
         leaves[kind] = {"a": even, "b": odd, "p": {x: added(s, odd.get(x)) for x, s in even.items()}}
 
-    def leaf_row(kind, sub, i, rows):
-        acc = [None] * rows
-        seen = {}
+    def leaf_rows(kind, sub, counts):
+        acc = {i: [None] * count for i, count in counts.items()}
+        mine = {}
         for (i2, m2), slot in leaves[kind][sub].items():
-            s = stage[slot]
-            for m in range(rows):
-                key = i + i2, m + m2
-                place = PLAN.two.get((kind, sub, *key))
-                if place is None:
-                    continue
-                if key not in seen:
-                    seen[key] = table[n, place]
-                v = seen[key] * s
-                acc[m] = v if acc[m] is None else acc[m] + v
+            mine.setdefault(i2, []).append((m2, slot))
+        loaded = {}
+        for top in sorted({i + i2 for i in counts for i2 in mine}):
+            seen = {}
+            for i, count in counts.items():
+                for m2, slot in mine.get(top - i, ()):
+                    for m in range(count):
+                        place = PLAN.two.get((kind, sub, top, m + m2))
+                        if place is None:
+                            continue
+                        if slot not in loaded:
+                            loaded[slot] = stage[slot]
+                        if m + m2 not in seen:
+                            seen[m + m2] = table[n, place]
+                        v = seen[m + m2] * loaded[slot]
+                        acc[i][m] = v if acc[i][m] is None else acc[i][m] + v
         return acc
 
-    def row_of(kind, i, count):
-        evens, odds = (count + 1) // 2, count // 2
-        p = leaf_row(kind, "p", i, evens)
-        a = leaf_row(kind, "a", i, evens)
-        b = leaf_row(kind, "b", i, odds) if odds else []
-        out = [None] * count
-        for m in range(evens):
-            out[2 * m] = a[m] if p[m] is None else p[m] + a[m]
-        for m in range(odds):
-            out[2 * m + 1] = p[m] + b[m]
+    def rows_of(kind, counts):
+        evens, odds = ({i: (count + e) // 2 for i, count in counts.items()} for e in (1, 0))
+        p = leaf_rows(kind, "p", evens)
+        a = leaf_rows(kind, "a", evens)
+        b = leaf_rows(kind, "b", odds)
+        out = {i: [None] * count for i, count in counts.items()}
+        for i in counts:
+            for m in range(evens[i]):
+                out[i][2 * m] = a[i][m] if p[i][m] is None else p[i][m] + a[i][m]
+            for m in range(odds[i]):
+                out[i][2 * m + 1] = p[i][m] + b[i][m]
         return out
 
-    for i in range(ORDER + 1):
-        count = ORDER + 1 - i
-        p = row_of("p", i, count)
-        a = row_of("a", i, count)
-        b = row_of("b", i, count - 1) if count > 1 else []
-        for j in range(count):
-            finish(LOWER[i, j, 0], a[j] if p[j] is None else p[j] + a[j])
-        for j in range(count - 1):
-            finish(LOWER[i, j, 1], p[j] + b[j])
+    left = list(range(ORDER + 1))
+    while left:
+        group = [i for i in (left[0], left[0] + step) if i in left]
+        left = [i for i in left if i not in group]
+        counts = {i: ORDER + 1 - i for i in group}
+        p = rows_of("p", counts)
+        a = rows_of("a", counts)
+        for i in group:
+            for j in range(counts[i]):
+                finish(LOWER[i, j, 0], a[i][j] if p[i][j] is None else p[i][j] + a[i][j])
+        b = rows_of("b", {i: count - 1 for i, count in counts.items()})
+        for i in group:
+            for j in range(counts[i] - 1):
+                finish(LOWER[i, j, 1], p[i][j] + b[i][j])
 
 
 def contract_half(table, h, sbuf, stage, stage2, tbuf):
     row = lax.broadcasted_iota(jnp.int32, (8, 128), 0)
     for b in range(COMP):
-        stage[b] = sbuf[pl.ds(b, 8, stride=QS), :]
+        stage[b] = sbuf[pl.ds(b, 8, stride=COMP), :]
     for (i, j, c), b in LOWER.items():
         if i % 2 == 0:
-            v = sbuf[pl.ds(8 * QS + b, 8, stride=QS), :]
+            v = sbuf[pl.ds(8 * COMP + b, 8, stride=COMP), :]
             up = LOWER.get((i + 1, j, c))
-            up = jnp.zeros((8, 128), F32) if up is None else sbuf[pl.ds(4 * QS + up, 8, stride=QS), :]
+            up = jnp.zeros((8, 128), F32) if up is None else sbuf[pl.ds(4 * COMP + up, 8, stride=COMP), :]
             stage2[b] = jnp.where(row < 4, v, up)
 
     def finish(a, v):
@@ -322,22 +354,26 @@
     contract(table, 2 + h, stage2, True, finish2)
 
 
-def backward(tbuf, vhigh, vlow, ybuf):
-    t = jnp.concatenate([tbuf[HALF * (2 * kc + r) : HALF * (2 * kc + r) + MROWS, :] for r in range(2) for kc in range(3)], axis=1)
-    high, low = split(t)
-    dot = functools.partial(jnp.dot, preferred_element_type=F32)
-    ybuf[...] = dot(high, vhigh[...]) + dot(low, vhigh[...]) + dot(high, vlow[...])
-
-
-def scatter_columns(ybuf, rest, msg, h, off):
+def backward(tbuf, whigh, wlow, thigh, tlow, ybuf):
     for r in range(2):
+        for kc in range(3):
+            row = (2 * kc + r) * HALF
+            put(thigh, tlow, 3 * r + kc, tbuf[row : row + 128, :].T, slice(0, 128))
+            put(thigh, tlow, 3 * r + kc, tbuf[row + 128 : row + 256, :].T, slice(128, 256))
+    ybuf[...] = product(whigh, wlow, thigh, tlow)
+
+
+def scatter_columns(ybuf, msg, h, off):
+    lane = lax.broadcasted_iota(jnp.int32, (NDEV, 128), 1)
+    rel = jnp.where(lane >= off, lane - off, lane - off + 128)
+    for r in range(2):
+        rest = None
         for z in range(ZL):
             at = (r * ZL + z) * NDEV
-            v = ybuf[0:128, at : at + NDEV].T
-            msg[h, pl.ds(2 * z + r, NDEV, stride=8), :] = pltpu.roll(v, off, 1)
-            rest[r, REST * z : REST * z + REST, :] = ybuf[128:HALF, at : at + NDEV]
-        v = pltpu.roll(rest[r].T, off, 1)
-        msg[h, pl.ds(6 + r, NDEV, stride=8), :] = v
+            msg[h, pl.ds(2 * z + r, NDEV, stride=8), :] = pltpu.roll(ybuf[at : at + NDEV, 0:128], off, 1)
+            v = pltpu.roll(ybuf[at : at + NDEV, 128:256], (off + REST * z) & 127, 1)
+            rest = v if z == 0 else jnp.where(rel >= REST * z, v, rest)
+        msg[h, pl.ds(6 + r, NDEV, stride=8), :] = rest
 
 
 def transpose_table(w, v):
@@ -349,7 +385,7 @@
 
 def kernel(
     planes_hbm, deriv_hbm, whigh_hbm, wlow_hbm, out_hbm,
-    plane, outp, deriv, whigh, wlow, vhigh, vlow, table, msg, got, msg2, got2, xbuf, sbuf, stage, stage2, tbuf, ybuf, rest,
+    plane, outp, deriv, whigh, wlow, vhigh, vlow, table, msg, got, msg2, got2, xhigh, xlow, sbuf, stage, stage2, tbuf, ybuf,
     load_sem, own_sem, send_sem, recv_sem, own_sem2, send_sem2, recv_sem2,
 ):
     me = lax.axis_index("grp") * INNER + lax.axis_index("dev")
@@ -363,23 +399,19 @@
         copy.start()
     barrier = pltpu.get_barrier_semaphore()
 
-    @pl.loop(1, NDEV)
-    def _(i):
-        d = (me + i) % NDEV
-        pl.semaphore_signal(barrier, inc=1, device_id=(d // INNER, d % INNER), device_id_type=MESH)
-
+    each_other(me, lambda d: pl.semaphore_signal(barrier, inc=1, device_id=device(d), device_id_type=MESH))
     plane[0:LEAD, :] = jnp.zeros((LEAD, 128), F32)
     plane[LEAD + ZL * ZROWS :, :] = jnp.zeros((16, 128), F32)
     loads[0].wait()
 
     for h in range(2):
 
-        @pl.loop(0, NDEV, unroll=4)
+        @pl.loop(0, NDEV, unroll=8)
         def _(d):
             pack(plane, msg, h, d)
 
-        if h == 0:
-            pl.semaphore_wait(barrier, NDEV - 1)
+    pl.semaphore_wait(barrier, NDEV - 1)
+    for h in range(2):
         send_all(me, msg, got, send_sem, recv_sem, h)
         own_copy(me, msg, got, own_sem, h).start()
     for copy in loads[1:]:
@@ -388,19 +420,16 @@
     prepare_tables(table)
     transpose_table(whigh, vhigh)
     transpose_table(wlow, vlow)
-    xbuf[:, 2 * QS :, :] = jnp.zeros((6, MROWS - 2 * QS, 128), F32)
-    rest[:, 3 * REST :, :] = jnp.zeros((2, 128 - 3 * REST, 128), F32)
-
     @pl.loop(0, 2)
     def _(h):
         off = column_start(me, h)[1]
         own_copy(me, msg, got, own_sem, h).wait()
         wait_bytes(got, recv_sem, h)
-        gather_columns(got, xbuf, h, off)
-        forward(xbuf, whigh, wlow, sbuf)
+        gather_columns(got, xhigh, xlow, h, off)
+        forward(xhigh, xlow, vhigh, vlow, sbuf)
         contract_half(table, h, sbuf, stage, stage2, tbuf)
-        backward(tbuf, vhigh, vlow, ybuf)
-        scatter_columns(ybuf, rest, msg2, h, off)
+        backward(tbuf, whigh, wlow, xhigh, xlow, ybuf)
+        scatter_columns(ybuf, msg2, h, off)
         send_all(me, msg2, got2, send_sem2, recv_sem2, h)
         own_copy(me, msg2, got2, own_sem2, h).start()
 
@@ -408,7 +437,7 @@
         own_copy(me, msg2, got2, own_sem2, h).wait()
         wait_bytes(got2, recv_sem2, h)
 
-        @pl.loop(0, NDEV, unroll=4)
+        @pl.loop(0, NDEV, unroll=8)
         def _(s):
             unpack(got2, outp, h, s)
 
@@ -444,13 +473,13 @@
             vmem((2, 8 * NDEV, 128), F32),
             vmem((2, 8 * NDEV, 128), F32),
             vmem((2, 8 * NDEV, 128), F32),
-            vmem((6, MROWS, 128), F32),
-            vmem((16 * QS, 128), F32),
+            vmem((2 * NZ, 256), BF16),
+            vmem((2 * NZ, 256), BF16),
+            vmem((16 * COMP, 128), F32),
             vmem((3 * COMP, 8, 128), F32),
             vmem((3 * COMP, 8, 128), F32),
             vmem((16 * COMP, 128), F32),
-            vmem((MROWS, 2 * NZ), F32),
-            vmem((2, 128, 128), F32),
+            vmem((2 * NZ, 256), F32),
             dma((4,)), dma((2,)), dma((2,)), dma((2,)), dma((2,)), dma((2,)), dma((2,)),
         ],
         compiler_params=pltpu.CompilerParams(

time: 55.4 us -> 52.2 us (0.942)
  Pallas kernels: 53 us -> 49.9 us
    pallas_call x1, Pallas kernels: 53 us -> 49.9 us  [on_device(): pl.pallas_call(kernel, out_shape=jax.ShapeDtypeStruct((ZL * ZROWS, 128),...]
where the time goes in v3:
time: 52.2 us; the launch traced here: 52.1 us
  Pallas kernels  49.9 us (96%)
  local copies, waits for them, and re-layouts  2.22 us (4%)
    pallas_call x1, Pallas kernels, on_device(): pl.pallas_call(kernel, out_shape=jax.ShapeDtypeStruct((ZL * ZROWS, 128),...  49.9 us
    unnamed x1, local copies, waits for them, and re-layouts  2.22 us

profile of v3, /device:TPU:1, one launch (start us, length us, event | category | flops | bytes accessed | tf_op | source)
XLA Modules:
  0.0 52.1 jit_solution(7466520662092588510)
XLA Ops:
  0.0 49.9 %m2l.1 = f32[1944,128]{1,0:T(8,128)} custom-call(f32[1944,128]{1,0:T(8,128)} %bitcast.15, f32[289,4,384]{2,1,0:T(4,128)} %bitcast.14, bf16[768,768]{1,0:T(8,128)(2,1)} %constant.4.clone.whigh_hbm, bf16[768,768]{1,0:T(8,128)(2,1)} %constant.5.clone.wlow_hbm), custom_call_target="tpu_custom_call" | custom-call | tf_op jit(solution)/shard_map/m2l/pallas_call | solution.py:458
  49.9 2.2 %copy.6 = f32[2,3,41472]{2,0,1:T(2,128)} copy(f32[2,3,41472]{2,0,1:T(2,128)} %bitcast.13) | data formatting | bytes 1990656

commit v4 on v3

--- a/solution.py
+++ b/solution.py
@@ -26,6 +26,7 @@
 REST = 34
 ZROWS = 648
 LEAD = 8
+OUT_ROWS = ZL * ZROWS + 8
 PLANE_ROWS = LEAD + ZL * ZROWS + 16
 
 
@@ -151,7 +152,7 @@
         if z:
             rest, rest2 = pltpu.roll(up2, 128 - REST * z, 1), pltpu.roll(up, 128 - REST * z, 1)
         v = jnp.where(first, top, jnp.where(second, jnp.where(here, rest, mid), rest2))
-        pltpu.store(plane.at[pl.ds(LEAD + z * ZROWS + 2 * tile, 8), :], v, mask=mask)
+        pltpu.store(plane.at[pl.ds(z * ZROWS + 2 * tile, 8), :], v, mask=mask)
 
 
 def each_other(me, action):
@@ -257,7 +258,7 @@
             sbuf[row + 128 : row + HALF, :] = out[at : at + 128, 128:256].T[:REST]
 
 
-def contract(table, n, stage, paired, finish):
+def contract(table, n, stage, paired, finish, hold, gate):
     step = 2 if paired else 1
     inputs = {}
     spare = [COMP]
@@ -322,18 +323,35 @@
         group = [i for i in (left[0], left[0] + step) if i in left]
         left = [i for i in left if i not in group]
         counts = {i: ORDER + 1 - i for i in group}
-        p = rows_of("p", counts)
-        a = rows_of("a", counts)
+        place = {}
         for i in group:
             for j in range(counts[i]):
-                finish(LOWER[i, j, 0], a[i][j] if p[i][j] is None else p[i][j] + a[i][j])
-        b = rows_of("b", {i: count - 1 for i, count in counts.items()})
-        for i in group:
-            for j in range(counts[i] - 1):
-                finish(LOWER[i, j, 1], p[i][j] + b[i][j])
-
-
-def contract_half(table, h, sbuf, stage, stage2, tbuf):
+                place[i, j] = len(place)
+        known = set()
+
+        @pl.when(gate)
+        def _():
+            p = rows_of("p", counts)
+            for (i, j), at in place.items():
+                if p[i][j] is not None:
+                    hold[at] = p[i][j]
+                    known.add((i, j))
+
+        @pl.when(gate)
+        def _():
+            a = rows_of("a", counts)
+            for (i, j), at in place.items():
+                finish(LOWER[i, j, 0], hold[at] + a[i][j] if (i, j) in known else a[i][j])
+
+        @pl.when(gate)
+        def _():
+            b = rows_of("b", {i: count - 1 for i, count in counts.items()})
+            for i in group:
+                for j in range(counts[i] - 1):
+                    finish(LOWER[i, j, 1], hold[place[i, j]] + b[i][j])
+
+
+def contract_half(table, h, sbuf, stage, stage2, tbuf, hold, gate):
     row = lax.broadcasted_iota(jnp.int32, (8, 128), 0)
     for b in range(COMP):
         stage[b] = sbuf[pl.ds(b, 8, stride=COMP), :]
@@ -350,8 +368,8 @@
     def finish2(a, v):
         tbuf[pl.ds(8 * COMP + a, 8, stride=COMP), :] = v + pltpu.roll(v, 4, 0)
 
-    contract(table, h, stage, False, finish)
-    contract(table, 2 + h, stage2, True, finish2)
+    contract(table, h, stage, False, finish, hold, gate)
+    contract(table, 2 + h, stage2, True, finish2, hold, gate)
 
 
 def backward(tbuf, whigh, wlow, thigh, tlow, ybuf):
@@ -384,8 +402,8 @@
 
 
 def kernel(
-    planes_hbm, deriv_hbm, whigh_hbm, wlow_hbm, out_hbm,
-    plane, outp, deriv, whigh, wlow, vhigh, vlow, table, msg, got, msg2, got2, xhigh, xlow, sbuf, stage, stage2, tbuf, ybuf,
+    planes_hbm, deriv_hbm, whigh_hbm, wlow_hbm, out,
+    plane, deriv, whigh, wlow, vhigh, vlow, table, msg, got, msg2, got2, xhigh, xlow, sbuf, stage, stage2, tbuf, hold, ybuf,
     load_sem, own_sem, send_sem, recv_sem, own_sem2, send_sem2, recv_sem2,
 ):
     me = lax.axis_index("grp") * INNER + lax.axis_index("dev")
@@ -427,7 +445,7 @@
         wait_bytes(got, recv_sem, h)
         gather_columns(got, xhigh, xlow, h, off)
         forward(xhigh, xlow, vhigh, vlow, sbuf)
-        contract_half(table, h, sbuf, stage, stage2, tbuf)
+        contract_half(table, h, sbuf, stage, stage2, tbuf, hold, me >= 0)
         backward(tbuf, whigh, wlow, xhigh, xlow, ybuf)
         scatter_columns(ybuf, msg2, h, off)
         send_all(me, msg2, got2, send_sem2, recv_sem2, h)
@@ -439,14 +457,11 @@
 
         @pl.loop(0, NDEV, unroll=8)
         def _(s):
-            unpack(got2, outp, h, s)
-
-    store = pltpu.make_async_copy(outp.at[pl.ds(LEAD, ZL * ZROWS), :], out_hbm, load_sem.at[0])
-    store.start()
+            unpack(got2, out, h, s)
+
     for h in range(2):
         wait_bytes(msg, send_sem, h)
         wait_bytes(msg2, send_sem2, h)
-    store.wait()
 
 
 def on_device(multipoles, derivatives):
@@ -457,11 +472,10 @@
     vmem, dma = pltpu.VMEM, pltpu.SemaphoreType.DMA
     out = pl.pallas_call(
         kernel,
-        out_shape=jax.ShapeDtypeStruct((ZL * ZROWS, 128), F32),
+        out_shape=jax.ShapeDtypeStruct((OUT_ROWS, 128), F32),
         in_specs=[pl.BlockSpec(memory_space=pl.ANY)] * 4,
-        out_specs=pl.BlockSpec(memory_space=pl.ANY),
+        out_specs=pl.BlockSpec(memory_space=pltpu.VMEM),
         scratch_shapes=[
-            vmem((PLANE_ROWS, 128), F32),
             vmem((PLANE_ROWS, 128), F32),
             vmem((289, 4, NZ), F32),
             vmem((2 * NZ, 2 * NZ), BF16),
@@ -479,15 +493,16 @@
             vmem((3 * COMP, 8, 128), F32),
             vmem((3 * COMP, 8, 128), F32),
             vmem((16 * COMP, 128), F32),
+            vmem((24, 8, 128), F32),
             vmem((2 * NZ, 256), F32),
             dma((4,)), dma((2,)), dma((2,)), dma((2,)), dma((2,)), dma((2,)), dma((2,)),
         ],
         compiler_params=pltpu.CompilerParams(
-            collective_id=0, has_side_effects=True, vmem_limit_bytes=60 * 1024 * 1024
+            collective_id=0, has_side_effects=True, vmem_limit_bytes=54000000
         ),
         name="m2l",
     )(planes, deriv, jnp.asarray(high), jnp.asarray(low))
-    out = jnp.transpose(out.reshape(ZL, COLS, 2, 128), (0, 2, 1, 3)).reshape(ZL, 2, COLS * 128)
+    out = jnp.transpose(out[: ZL * ZROWS].reshape(ZL, COLS, 2, 128), (0, 2, 1, 3)).reshape(ZL, 2, COLS * 128)
     return jnp.transpose(out, (1, 0, 2))
 
 

time: 52.2 us -> 49.8 us (0.954)
  Pallas kernels: 49.9 us -> 47.4 us
    pallas_call x1, Pallas kernels: 49.9 us -> 47.4 us  [on_device(): pl.pallas_call(kernel, out_shape=jax.ShapeDtypeStruct((OUT_ROWS, 128), F3...]
    slice x0 -> x1, local copies, waits for them, and re-layouts: none -> 1.01 us  [on_device(): out[:ZL * ZROWS].reshape(ZL, COLS, 2, 128)]
    unnamed x1 -> x2, local copies, waits for them, and re-layouts: 2.22 us -> 1.21 us
where the time goes in v4:
time: 49.8 us; the launch traced here: 49.6 us
  Pallas kernels  47.4 us (95%)
  local copies, waits for them, and re-layouts  2.22 us (4%)
    pallas_call x1, Pallas kernels, on_device(): pl.pallas_call(kernel, out_shape=jax.ShapeDtypeStruct((OUT_ROWS, 128), F3...  47.4 us
    unnamed x2, local copies, waits for them, and re-layouts  1.21 us
    slice x1, local copies, waits for them, and re-layouts, on_device(): out[:ZL * ZROWS].reshape(ZL, COLS, 2, 128)  1.01 us

profile of v4, /device:TPU:1, one launch (start us, length us, event | category | flops | bytes accessed | tf_op | source)
XLA Modules:
  0.0 49.6 jit_solution(9990063717414933226)
XLA Ops:
  0.0 0.0 copy-start
  0.0 1.2 %copy-done = f32[2,3,41472]{2,0,1:T(2,128)S(1)} copy-done((f32[2,3,41472]{2,0,1:T(2,128)S(1)}, f32[2,3,41472]{2,0,1:T(2,128)}, u32[]{:S(2)}) %copy-start) | copy-done | bytes 995352
  1.2 47.4 %m2l.1 = f32[1952,128]{1,0:T(8,128)S(1)} custom-call(f32[1944,128]{1,0:T(8,128)S(1)} %bitcast.13, f32[289,4,384]{2,1,0:T(4,128)} %bitcast.14, bf16[768,768]{1,0:T(8,128)(2,1)} %constant.4.clone.whigh_hbm, bf16[768,768]{1,0:T(8,128)(2,1)} %constant.5.clone.wlow_hbm), custom_call_target="tpu_custom_call" | custom-call | tf_op jit(solution)/shard_map/m2l/pallas_call | solution.py:473
  48.6 1.0 %slice.3 = f32[1944,128]{1,0:T(8,128)} slice(f32[1952,128]{1,0:T(8,128)S(1)} %m2l.1), slice={[0:1944], [0:128]} | slice | bytes 1990656 | tf_op jit(solution)/shard_map/slice | solution.py:505
Async XLA Ops:
  0.0 1.2 %copy-start = (f32[2,3,41472]{2,0,1:T(2,128)S(1)}, f32[2,3,41472]{2,0,1:T(2,128)}, u32[]{:S(2)}) copy-start(f32[2,3,41472]{2,0,1:T(2,128)} %param.4) | copy-start | bytes 2985988

commit v5 on v4

--- a/solution.py
+++ b/solution.py
@@ -24,6 +24,8 @@
 COLS = 324
 HALF = 162
 REST = 34
+MROWS = 168
+ROOT = math.sqrt(3.0) / 2
 ZROWS = 648
 LEAD = 8
 OUT_ROWS = ZL * ZROWS + 8
@@ -93,15 +95,27 @@
 PLAN = Plan()
 
 
-def dft_table():
-    z = (3 * np.arange(NDEV)[None, :] + np.arange(ZL)[:, None]).reshape(-1)
-    k = np.arange(NZ)
-    angle = 2.0 * np.pi / NZ * (z[:, None] * k[None, :] % NZ)
+def dft_tables():
+    n = np.arange(NDEV)
+    angle = 2.0 * np.pi / NDEV * (n[:, None] * n[None, :] % NDEV)
     c, s = np.cos(angle) / math.sqrt(NZ), np.sin(angle) / math.sqrt(NZ)
-    w = np.block([[c, -s], [s, c]])
-    high = w.astype(ml_dtypes.bfloat16)
-    low = (w - high.astype(np.float64)).astype(ml_dtypes.bfloat16)
-    return high, low
+    out = []
+    for w in (np.block([[c, -s], [s, c]]), np.block([[c, s], [-s, c]])):
+        high = w.astype(ml_dtypes.bfloat16)
+        out += [high, (w - high.astype(np.float64)).astype(ml_dtypes.bfloat16)]
+    rows = np.concatenate(out + turn_rows())
+    return np.pad(rows, ((0, 5120 - len(rows)), (0, 0)))
+
+
+def turn_rows():
+    angle = 2.0 * np.pi / NZ * np.arange(NDEV)
+    left = np.zeros((16, 256))
+    left[:4, :NDEV] = [f(z * angle) for z in (1, 2) for f in (np.cos, np.sin)]
+    out = []
+    for _ in range(3):
+        out.append(left.astype(ml_dtypes.bfloat16))
+        left = left - out[-1].astype(np.float64)
+    return out
 
 
 def split(x):
@@ -228,34 +242,49 @@
             table[n, slot] = -table[n, y] if x is None else table[n, x] - table[n, y]
 
 
-def put(high, low, n, v, lanes):
-    h, l = split(v)
-    high[128 * n : 128 * n + 128, lanes] = h
-    low[128 * n : 128 * n + 128, lanes] = l
-
-
-def gather_columns(got, xhigh, xlow, h, off):
+def gather_columns(got, xt, h, off):
+    back = (128 - off) & 127
     for r in range(2):
-        rest = got[h, pl.ds(6 + r, NDEV, stride=8), :]
+        lanes = slice(128 * r, 128 * r + 128)
         for z in range(ZL):
             v = got[h, pl.ds(2 * z + r, NDEV, stride=8), :]
-            put(xhigh, xlow, r * ZL + z, pltpu.roll(v, (128 - off) & 127, 1), slice(0, 128))
-            v = pltpu.roll(rest, (256 - off - REST * z) & 127, 1)
-            put(xhigh, xlow, r * ZL + z, v, slice(128, 256))
-
-
-def product(whigh, wlow, high, low):
+            xt[MROWS * z : MROWS * z + 128, lanes] = pltpu.roll(v, back, 1).T
+        v = pltpu.roll(got[h, pl.ds(6 + r, NDEV, stride=8), :], back, 1).T
+        for z in range(ZL):
+            xt[MROWS * z + 128 : MROWS * z + HALF, lanes] = v[REST * z : REST * z + REST]
+
+
+def product(x, w, first):
+    high, low = split(x)
     dot = functools.partial(jnp.dot, preferred_element_type=F32)
-    return dot(whigh[...], high[...]) + dot(whigh[...], low[...]) + dot(wlow[...], high[...])
-
-
-def forward(xhigh, xlow, vhigh, vlow, sbuf):
-    out = product(vhigh, vlow, xhigh, xlow)
-    for r in range(2):
-        for kc in range(3):
-            at, row = 128 * (3 * r + kc), (2 * kc + r) * HALF
-            sbuf[row : row + 128, :] = out[at : at + 128, 0:128].T
-            sbuf[row + 128 : row + HALF, :] = out[at : at + 128, 128:256].T[:REST]
+    whigh, wlow = w[256 * first : 256 * first + 256, :], w[256 * first + 256 : 256 * first + 512, :]
+    return dot(high, whigh) + dot(low, whigh) + dot(high, wlow)
+
+
+def turned(turn, z, re, im, sign):
+    if z == 0:
+        return re, im
+    c, s = turn[2 * z - 2 : 2 * z - 1, :], turn[2 * z - 1 : 2 * z, :] * sign
+    return re * c - im * s, im * c + re * s
+
+
+def triple(a, b, c, sign):
+    sums = b[0] + c[0], b[1] + c[1]
+    v = (b[0] - c[0]) * (ROOT * sign), (b[1] - c[1]) * (ROOT * sign)
+    u = a[0] - 0.5 * sums[0], a[1] - 0.5 * sums[1]
+    return (a[0] + sums[0], a[1] + sums[1]), (u[0] - v[1], u[1] + v[0]), (u[0] + v[1], u[1] - v[0])
+
+
+def forward(xt, w, turn, sbuf):
+    g = product(xt[...], w, 0)
+    parts = []
+    for z in range(ZL):
+        at = MROWS * z
+        parts.append(turned(turn, z, g[at : at + MROWS, 0:128], g[at : at + MROWS, 128:256], -1.0))
+    for kc, value in enumerate(triple(*parts, -1.0)):
+        for r in range(2):
+            row = (2 * kc + r) * HALF
+            sbuf[row : row + HALF, :] = value[r][:HALF]
 
 
 def contract(table, n, stage, paired, finish, hold, gate):
@@ -372,46 +401,36 @@
     contract(table, 2 + h, stage2, True, finish2, hold, gate)
 
 
-def backward(tbuf, whigh, wlow, thigh, tlow, ybuf):
+def backward(tbuf, w, turn, ybuf):
+    parts = []
+    for kc in range(3):
+        rows = [(2 * kc + r) * HALF for r in range(2)]
+        parts.append(tuple(tbuf[row : row + MROWS, :] for row in rows))
+    x = [turned(turn, z, *value, 1.0) for z, value in enumerate(triple(*parts, 1.0))]
+    x = jnp.concatenate([jnp.concatenate(v, axis=1) for v in x], axis=0)
+    ybuf[...] = product(x, w, 2)
+
+
+def scatter_columns(ybuf, rest, msg, h, off):
     for r in range(2):
-        for kc in range(3):
-            row = (2 * kc + r) * HALF
-            put(thigh, tlow, 3 * r + kc, tbuf[row : row + 128, :].T, slice(0, 128))
-            put(thigh, tlow, 3 * r + kc, tbuf[row + 128 : row + 256, :].T, slice(128, 256))
-    ybuf[...] = product(whigh, wlow, thigh, tlow)
-
-
-def scatter_columns(ybuf, msg, h, off):
-    lane = lax.broadcasted_iota(jnp.int32, (NDEV, 128), 1)
-    rel = jnp.where(lane >= off, lane - off, lane - off + 128)
-    for r in range(2):
-        rest = None
+        lanes = slice(128 * r, 128 * r + 128)
         for z in range(ZL):
-            at = (r * ZL + z) * NDEV
-            msg[h, pl.ds(2 * z + r, NDEV, stride=8), :] = pltpu.roll(ybuf[at : at + NDEV, 0:128], off, 1)
-            v = pltpu.roll(ybuf[at : at + NDEV, 128:256], (off + REST * z) & 127, 1)
-            rest = v if z == 0 else jnp.where(rel >= REST * z, v, rest)
-        msg[h, pl.ds(6 + r, NDEV, stride=8), :] = rest
-
-
-def transpose_table(w, v):
-    for x in range(6):
-        for y in range(6):
-            block = w[128 * x : 128 * x + 128, 128 * y : 128 * y + 128].astype(F32)
-            v[128 * y : 128 * y + 128, 128 * x : 128 * x + 128] = block.T.astype(BF16)
+            at = MROWS * z
+            msg[h, pl.ds(2 * z + r, NDEV, stride=8), :] = pltpu.roll(ybuf[at : at + 128, lanes].T, off, 1)
+            rest[r, REST * z : REST * z + REST, :] = ybuf[at + 128 : at + HALF, lanes]
+        msg[h, pl.ds(6 + r, NDEV, stride=8), :] = pltpu.roll(rest[r].T, off, 1)
 
 
 def kernel(
-    planes_hbm, deriv_hbm, whigh_hbm, wlow_hbm, out,
-    plane, deriv, whigh, wlow, vhigh, vlow, table, msg, got, msg2, got2, xhigh, xlow, sbuf, stage, stage2, tbuf, hold, ybuf,
+    planes_hbm, deriv_hbm, w_hbm, out,
+    plane, deriv, w, turn, table, msg, got, msg2, got2, xt, sbuf, stage, stage2, tbuf, hold, ybuf, rest,
     load_sem, own_sem, send_sem, recv_sem, own_sem2, send_sem2, recv_sem2,
 ):
     me = lax.axis_index("grp") * INNER + lax.axis_index("dev")
     loads = [
         pltpu.make_async_copy(planes_hbm, plane.at[pl.ds(LEAD, ZL * ZROWS), :], load_sem.at[0]),
         pltpu.make_async_copy(deriv_hbm, deriv, load_sem.at[1]),
-        pltpu.make_async_copy(whigh_hbm, whigh, load_sem.at[2]),
-        pltpu.make_async_copy(wlow_hbm, wlow, load_sem.at[3]),
+        pltpu.make_async_copy(w_hbm.at[pl.ds(0, 1072), :], w, load_sem.at[2]),
     ]
     for copy in loads:
         copy.start()
@@ -436,18 +455,20 @@
         copy.wait()
     prepare_base(deriv, table)
     prepare_tables(table)
-    transpose_table(whigh, vhigh)
-    transpose_table(wlow, vlow)
+    small = [w[1024 + 16 * n : 1040 + 16 * n, 0:128].astype(F32) for n in range(3)]
+    turn[...] = small[0] + (small[1] + small[2])
+    xt[...] = jnp.zeros(xt.shape, F32)
+    rest[...] = jnp.zeros(rest.shape, F32)
     @pl.loop(0, 2)
     def _(h):
         off = column_start(me, h)[1]
         own_copy(me, msg, got, own_sem, h).wait()
         wait_bytes(got, recv_sem, h)
-        gather_columns(got, xhigh, xlow, h, off)
-        forward(xhigh, xlow, vhigh, vlow, sbuf)
+        gather_columns(got, xt, h, off)
+        forward(xt, w, turn, sbuf)
         contract_half(table, h, sbuf, stage, stage2, tbuf, hold, me >= 0)
-        backward(tbuf, whigh, wlow, xhigh, xlow, ybuf)
-        scatter_columns(ybuf, msg2, h, off)
+        backward(tbuf, w, turn, ybuf)
+        scatter_columns(ybuf, rest, msg2, h, off)
         send_all(me, msg2, got2, send_sem2, recv_sem2, h)
         own_copy(me, msg2, got2, own_sem2, h).start()
 
@@ -468,40 +489,37 @@
     planes = with_layout_constraint(multipoles.reshape(2, ZL, COLS, 128), Layout((1, 2, 0, 3)))
     planes = jnp.transpose(planes, (1, 2, 0, 3)).reshape(ZL * ZROWS, 128)
     deriv = jnp.transpose(derivatives, (2, 1, 0))
-    high, low = dft_table()
     vmem, dma = pltpu.VMEM, pltpu.SemaphoreType.DMA
     out = pl.pallas_call(
         kernel,
         out_shape=jax.ShapeDtypeStruct((OUT_ROWS, 128), F32),
-        in_specs=[pl.BlockSpec(memory_space=pl.ANY)] * 4,
+        in_specs=[pl.BlockSpec(memory_space=pl.ANY)] * 3,
         out_specs=pl.BlockSpec(memory_space=pltpu.VMEM),
         scratch_shapes=[
             vmem((PLANE_ROWS, 128), F32),
             vmem((289, 4, NZ), F32),
-            vmem((2 * NZ, 2 * NZ), BF16),
-            vmem((2 * NZ, 2 * NZ), BF16),
-            vmem((2 * NZ, 2 * NZ), BF16),
-            vmem((2 * NZ, 2 * NZ), BF16),
+            vmem((1072, 256), BF16),
+            vmem((16, 128), F32),
             vmem((4, PLAN.count, 8, 128), F32),
             vmem((2, 8 * NDEV, 128), F32),
             vmem((2, 8 * NDEV, 128), F32),
             vmem((2, 8 * NDEV, 128), F32),
             vmem((2, 8 * NDEV, 128), F32),
-            vmem((2 * NZ, 256), BF16),
-            vmem((2 * NZ, 256), BF16),
+            vmem((ZL * MROWS, 256), F32),
             vmem((16 * COMP, 128), F32),
             vmem((3 * COMP, 8, 128), F32),
             vmem((3 * COMP, 8, 128), F32),
             vmem((16 * COMP, 128), F32),
             vmem((24, 8, 128), F32),
-            vmem((2 * NZ, 256), F32),
+            vmem((ZL * MROWS, 256), F32),
+            vmem((2, 128, 128), F32),
             dma((4,)), dma((2,)), dma((2,)), dma((2,)), dma((2,)), dma((2,)), dma((2,)),
         ],
         compiler_params=pltpu.CompilerParams(
-            collective_id=0, has_side_effects=True, vmem_limit_bytes=54000000
+            collective_id=0, has_side_effects=True, vmem_limit_bytes=54300000
         ),
         name="m2l",
-    )(planes, deriv, jnp.asarray(high), jnp.asarray(low))
+    )(planes, deriv, jnp.asarray(dft_tables()))
     out = jnp.transpose(out[: ZL * ZROWS].reshape(ZL, COLS, 2, 128), (0, 2, 1, 3)).reshape(ZL, 2, COLS * 128)
     return jnp.transpose(out, (1, 0, 2))
 

time: 49.8 us -> 45.5 us (0.914)
  Pallas kernels: 47.4 us -> 43.2 us
    pallas_call x1, Pallas kernels: 47.4 us -> 43.2 us  [on_device(): pl.pallas_call(kernel, out_shape=jax.ShapeDtypeStruct((OUT_ROWS, 128), F3...]
where the time goes in v5:
time: 45.5 us; the launch traced here: 45.4 us
  Pallas kernels  43.2 us (95%)
  local copies, waits for them, and re-layouts  2.22 us (5%)
    pallas_call x1, Pallas kernels, on_device(): pl.pallas_call(kernel, out_shape=jax.ShapeDtypeStruct((OUT_ROWS, 128), F3...  43.2 us
    unnamed x2, local copies, waits for them, and re-layouts  1.21 us
    slice x1, local copies, waits for them, and re-layouts, on_device(): out[:ZL * ZROWS].reshape(ZL, COLS, 2, 128)  1.01 us

profile of v5, /device:TPU:1, one launch (start us, length us, event | category | flops | bytes accessed | tf_op | source)
XLA Modules:
  0.0 45.4 jit_solution(16334703734805940243)
XLA Ops:
  0.0 0.0 copy-start
  0.0 1.2 %copy-done = f32[2,3,41472]{2,0,1:T(2,128)S(1)} copy-done((f32[2,3,41472]{2,0,1:T(2,128)S(1)}, f32[2,3,41472]{2,0,1:T(2,128)}, u32[]{:S(2)}) %copy-start) | copy-done | bytes 995352
  1.2 43.2 %m2l.1 = f32[1952,128]{1,0:T(8,128)S(1)} custom-call(f32[1944,128]{1,0:T(8,128)S(1)} %bitcast.13, f32[289,4,384]{2,1,0:T(4,128)} %bitcast.14, bf16[5120,256]{1,0:T(8,128)(2,1)} %constant.2.clone.w_hbm), custom_call_target="tpu_custom_call" | custom-call | tf_op jit(solution)/shard_map/m2l/pallas_call | solution.py:493
  44.4 1.0 %slice.3 = f32[1944,128]{1,0:T(8,128)} slice(f32[1952,128]{1,0:T(8,128)S(1)} %m2l.1), slice={[0:1944], [0:128]} | slice | bytes 1990656 | tf_op jit(solution)/shard_map/slice | solution.py:523
Async XLA Ops:
  0.0 1.2 %copy-start = (f32[2,3,41472]{2,0,1:T(2,128)S(1)}, f32[2,3,41472]{2,0,1:T(2,128)}, u32[]{:S(2)}) copy-start(f32[2,3,41472]{2,0,1:T(2,128)} %param.3) | copy-start | bytes 2985988

commit v6 on v5

--- a/solution.py
+++ b/solution.py
@@ -492,7 +492,7 @@
     vmem, dma = pltpu.VMEM, pltpu.SemaphoreType.DMA
     out = pl.pallas_call(
         kernel,
-        out_shape=jax.ShapeDtypeStruct((OUT_ROWS, 128), F32),
+        out_shape=pltpu.VMEM((OUT_ROWS, 128), F32),
         in_specs=[pl.BlockSpec(memory_space=pl.ANY)] * 3,
         out_specs=pl.BlockSpec(memory_space=pltpu.VMEM),
         scratch_shapes=[
@@ -516,7 +516,7 @@
             dma((4,)), dma((2,)), dma((2,)), dma((2,)), dma((2,)), dma((2,)), dma((2,)),
         ],
         compiler_params=pltpu.CompilerParams(
-            collective_id=0, has_side_effects=True, vmem_limit_bytes=54300000
+            collective_id=0, has_side_effects=True, vmem_limit_bytes=55000000
         ),
         name="m2l",
     )(planes, deriv, jnp.asarray(dft_tables()))

time: 45.5 us -> 43.9 us (0.965)
  local copies, waits for them, and re-layouts: 2.22 us -> 1.01 us
    unnamed x2 -> x0, local copies, waits for them, and re-layouts: 1.21 us -> none
where the time goes in v6:
time: 43.9 us; the launch traced here: 43.8 us
  Pallas kernels  42.8 us (97%)
  local copies, waits for them, and re-layouts  1.01 us (2%)
    pallas_call x1, Pallas kernels, on_device(): pl.pallas_call(kernel, out_shape=pltpu.VMEM((OUT_ROWS, 128), F32), in_spe...  42.8 us
    slice x1, local copies, waits for them, and re-layouts, on_device(): out[:ZL * ZROWS].reshape(ZL, COLS, 2, 128)  1.01 us

profile of v6, /device:TPU:1, one launch (start us, length us, event | category | flops | bytes accessed | tf_op | source)
XLA Modules:
  0.0 43.8 jit_solution(17667537952850653174)
XLA Ops:
  0.0 42.8 %m2l.1 = f32[1952,128]{1,0:T(8,128)S(1)} custom-call(f32[1944,128]{1,0:T(8,128)} %bitcast.14, f32[289,4,384]{2,1,0:T(4,128)} %bitcast.13, bf16[5120,256]{1,0:T(8,128)(2,1)} %constant.2.clone.w_hbm), custom_call_target="tpu_custom_call" | custom-call | tf_op jit(solution)/shard_map/m2l/pallas_call | solution.py:493
  42.8 1.0 %slice.3 = f32[1944,128]{1,0:T(8,128)} slice(f32[1952,128]{1,0:T(8,128)S(1)} %m2l.1), slice={[0:1944], [0:128]} | slice | bytes 1990656 | tf_op jit(solution)/shard_map/slice | solution.py:523

commit v7 on v6

--- a/solution.py
+++ b/solution.py
@@ -175,9 +175,9 @@
     @pl.loop(0, (NDEV - 2) // step)
     def _(t):
         for u in range(step):
-            action((me + step * t + u + 1) & (NDEV - 1))
-
-    action((me + NDEV - 1) & (NDEV - 1))
+            action((me + 37 * (step * t + u + 1)) & (NDEV - 1))
+
+    action((me - 37) & (NDEV - 1))
 
 
 def device(d):

time: 43.9 us -> 43.4 us (0.989)
  Pallas kernels: 42.8 us -> 42.3 us
    pallas_call x1, Pallas kernels: 42.8 us -> 42.3 us  [on_device(): pl.pallas_call(kernel, out_shape=pltpu.VMEM((OUT_ROWS, 128), F32), in_spe...]
where the time goes in v7:
time: 43.4 us; the launch traced here: 43.3 us
  Pallas kernels  42.3 us (97%)
  local copies, waits for them, and re-layouts  1.01 us (2%)
    pallas_call x1, Pallas kernels, on_device(): pl.pallas_call(kernel, out_shape=pltpu.VMEM((OUT_ROWS, 128), F32), in_spe...  42.3 us
    slice x1, local copies, waits for them, and re-layouts, on_device(): out[:ZL * ZROWS].reshape(ZL, COLS, 2, 128)  1.01 us

profile of v7, /device:TPU:1, one launch (start us, length us, event | category | flops | bytes accessed | tf_op | source)
XLA Modules:
  0.0 43.3 jit_solution(657758592830414597)
XLA Ops:
  0.0 42.3 %m2l.1 = f32[1952,128]{1,0:T(8,128)S(1)} custom-call(f32[1944,128]{1,0:T(8,128)} %bitcast.14, f32[289,4,384]{2,1,0:T(4,128)} %bitcast.13, bf16[5120,256]{1,0:T(8,128)(2,1)} %constant.2.clone.w_hbm), custom_call_target="tpu_custom_call" | custom-call | tf_op jit(solution)/shard_map/m2l/pallas_call | solution.py:493
  42.3 1.0 %slice.3 = f32[1944,128]{1,0:T(8,128)} slice(f32[1952,128]{1,0:T(8,128)S(1)} %m2l.1), slice={[0:1944], [0:128]} | slice | bytes 1990656 | tf_op jit(solution)/shard_map/slice | solution.py:523
